TPU v7x, 32 devices: a whole 2x2x4 slice. The times are simulated.
32 devices in a mesh: client: 4 (over x, core), blk: 8 (over z, y).
Axes of the slice: x: 2, y: 2, z: 4, core: 2. Of those that a mesh axis runs over, the one named last changes fastest.
Arguments:
- activations: bfloat16 [8, 2, 8, 8, 1280], P('client', None, 'blk'), may hold values from -6 to 6
- sample_count: int32 [8], replicated, may hold values from 1 to 2, as said below
- client_weights: bfloat16 [8, 11520, 1280], P('client', 'blk'), may hold values from -6 to 6
Outputs:
- merged_gram: float32 [11520, 11520], P(('blk', 'client'))
- merged_rhs: float32 [11520, 1280], P(('blk', 'client'))
Inputs may be any that keep to these rules, and one draw needn't show every extreme that they name: `sample_count`: some client has all 2 slots live in every draw.
All inputs are finite; a program needn't handle non-finite values.
Results may differ from a plain program's by a relative error of at most 0.0029.
Values may be sent and summed in bfloat16 or wider, within the bound.
A program may use at most 192 MiB of HBM per device.

v0:
```python
import jax
import jax.numpy as jnp
import numpy as np
from jax import lax
from jax.sharding import PartitionSpec as P

keep_off = 0.9


def patch_rows(images):
    groups, slots, img_height, img_width, channel_count = images.shape
    padded = jnp.pad(images, [(0, 0), (0, 0), (1, 1), (1, 1), (0, 0)])
    shifted = [
        padded[:, :, row_off : row_off + img_height, col_off : col_off + img_width, :]
        for row_off in range(3)
        for col_off in range(3)
    ]
    joined = jnp.concatenate(shifted, axis=-1)
    joined = joined.reshape(groups, slots * img_height * img_width, 9 * channel_count)
    column_order = (
        np.arange(9 * channel_count).reshape(9, channel_count).T.reshape(-1).astype(np.int32)
    )
    return jnp.take(joined, jnp.asarray(column_order), axis=2)


def body(activations, sample_count, client_weights):
    blk_count = lax.axis_size("blk")
    client_here = lax.axis_index("client")
    blk_here = lax.axis_index("blk")
    group_size = activations.shape[0]
    slot_count = activations.shape[1]
    pixel_count = activations.shape[2] * blk_count * activations.shape[3]
    client_total = sample_count.shape[0]
    mine_counts = lax.dynamic_slice_in_dim(sample_count, client_here * group_size, group_size)
    my_scale = 1.0 / (client_total * mine_counts.astype(jnp.float32) * pixel_count)
    live = lax.broadcasted_iota(jnp.int32, (group_size, slot_count), 1) < mine_counts[:, None]
    masked = jnp.where(live[:, :, None, None, None], activations, jnp.zeros_like(activations))
    tiles = lax.all_to_all(masked, "blk", split_axis=4, concat_axis=2, tiled=True)
    own_patch = patch_rows(tiles)
    tile_rows = own_patch.shape[2]
    partial_out = jnp.einsum(
        "irk,iko->rio", own_patch, client_weights, preferred_element_type=jnp.float32
    )
    summed_out = lax.psum(partial_out, "blk")
    out_bf = summed_out.astype(jnp.bfloat16)
    cross = jnp.einsum("irk,rio->iko", own_patch, out_bf, preferred_element_type=jnp.float32)
    diag_part = jnp.sum(jnp.square(own_patch.astype(jnp.float32)), axis=1)
    rhs_terms = keep_off * cross + (1.0 - keep_off) * diag_part[:, :, None] * client_weights.astype(
        jnp.float32
    )
    rhs_rows = jnp.sum(my_scale[:, None, None] * rhs_terms, axis=0)
    their_patch = patch_rows(lax.all_gather(tiles, "blk", axis=4, tiled=True))
    products = jnp.einsum(
        "irk,irl->ikl", own_patch, their_patch, preferred_element_type=jnp.float32
    )
    gram_rows = jnp.sum(my_scale[:, None, None] * products, axis=0)
    gram_mine, rhs_mine = (
        lax.psum_scatter(gram_rows, "client", scatter_dimension=0, tiled=True),
        lax.psum_scatter(rhs_rows, "client", scatter_dimension=0, tiled=True),
    )
    mine_rows = gram_mine.shape[0]
    first_diag = blk_here * tile_rows + client_here * mine_rows
    on_diag = (
        lax.broadcasted_iota(jnp.int32, gram_mine.shape, 1)
        == lax.broadcasted_iota(jnp.int32, gram_mine.shape, 0) + first_diag
    )
    gram_out = jnp.where(on_diag, gram_mine, keep_off * gram_mine)
    return (gram_out, rhs_mine)


def solution(mesh):
    in_specs = (P("client", None, "blk", None, None), P(), P("client", "blk", None))
    out_specs = (P(("blk", "client"), None), P(("blk", "client"), None))
    return jax.shard_map(body, mesh=mesh, in_specs=in_specs, out_specs=out_specs, check_vma=False)
```

profile of v0, /device:TPU:0, one launch (start us, length us, event | category | flops | bytes accessed | tf_op | source)
XLA Modules:
  0.0 1007.8 jit_solution(14062568862968788323)
XLA Ops:
  7.2 0.7 multiply_divide_fusion
  7.9 0.1 iota_compare_fusion.1
  8.0 1.0 broadcast_select_fusion
  8.9 1.6 copy.104
  10.6 2.0 reshape.72
  12.6 7.3 all-to-all-start
  19.9 0.0 reduce-scatter.3.cloned.1.call-start
  19.9 0.7 pad_clamp_fusion.1
  20.6 6.3 all-to-all-done
  26.9 1.5 reshape.73
  28.4 2.1 copy.132
  30.5 0.0 copy-start.1
  30.6 1.7 copy.133
  32.3 0.1 pad_slice_fusion.8
  32.4 0.1 copy.115
  32.5 0.1 constant_dynamic-update-slice_fusion.8
  32.6 0.1 copy.116
  32.8 0.1 copy.117
  32.9 0.1 copy.118
  33.1 0.1 copy.119
  33.2 0.1 copy.120
  33.4 0.1 copy.121
  33.5 0.1 copy.122
  33.7 0.1 copy.123
  33.8 0.1 constant_dynamic-update-slice_fusion.7
  33.9 0.1 constant_dynamic-update-slice_fusion.6
  34.0 0.1 constant_dynamic-update-slice_fusion.5
  34.0 0.1 constant_dynamic-update-slice_fusion.4
  34.1 0.1 constant_dynamic-update-slice_fusion.3
  34.2 0.1 constant_dynamic-update-slice_fusion.2
  34.3 0.1 constant_dynamic-update-slice_fusion.1
  34.3 0.0 copy-done.1
  34.3 0.1 constant_dynamic-update-slice_fusion
  34.4 5.1 gather_fusion
  39.6 2.5 multiply_reduce_fusion.1
  42.1 4.4 convolution_bitcast_fusion
  46.4 76.6 %all-reduce.3 = bf16[128,2,1280]{2,0,1:T(8,128)(2,1)S(1)} all-reduce(f32[128,2,1280]{2,0,1:T(8,128)S(1)} %convolution_bitcast_fusion), channel_id=1, replica_groups=mesh['client'=4,'blk'=8] {'blk'}, use_global_device_ids=true, to_apply=%region_2.3 | all-reduce | flops 327680 | bytes 1966080 | tf_op jit(solution)/shard_map/psum | solution.py:44
  123.1 0.3 copy.131
  123.4 8.9 fusion.3
  132.3 0.0 copy-start.3
  132.3 0.0 copy-start.2
  132.3 0.0 reduce-scatter.3.cloned.1.call-update
  132.3 0.8 copy-done.3
  133.1 0.1 copy-done.2
  133.2 1.8 copy.124
  135.1 186.0 %all-gather = bf16[2,2,8,1,8,1280]{4,2,3,1,0,5:T(8,128)(2,1)} all-gather(bf16[2,2,8,1,8,160]{4,2,3,1,0,5:T(8,128)(2,1)S(1)} %copy.124), channel_id=2, replica_groups=mesh['client'=4,'blk'=8] {'blk'}, dimensions={5}, use_global_device_ids=true | all-gather | bytes 737280 | tf_op jit(solution)/shard_map/all_gather | solution.py:52
  321.0 9.1 copy.125
  330.1 0.1 fusion.4
  330.3 0.1 fusion.6
  330.4 0.2 fusion.7
  330.6 0.2 fusion.8
  330.8 0.1 fusion.9
  331.0 0.1 fusion.11
  331.1 0.0 copy-start
  331.1 2.6 copy-done
  333.7 15.4 %copy.126 = bf16[2,128,11520]{1,0,2:T(2,128)(2,1)} copy(bf16[2,128,11520]{2,1,0:T(8,128)(2,1)} %bitcast.40) | data formatting | bytes 11796480 | tf_op jit(solution)/shard_map/reshape | solution.py:19
  349.1 31.9 %gather_fusion.1 = bf16[11520,2,128]{2,1,0:T(2,128)(2,1)} fusion(bf16[2,128,11520]{1,0,2:T(2,128)(2,1)} %copy.126, s32[12288]{0:T(1024)S(1)} %pad_clamp_fusion), kind=kCustom, calls=%fused_computation.1 | custom fusion | bytes 11842560 | tf_op jit(solution)/shard_map/jit(_take)/gather | solution.py:23
  381.0 43.8 %multiply_reduce_fusion = f32[1440,11520]{1,0:T(8,128)} fusion(f32[2]{0:T(128)S(1)} %get-tuple-element.2, bf16[2,128,11520]{1,0,2:T(2,128)(2,1)} %bitcast.41, bf16[2,128,1440]{1,0,2:T(2,128)(2,1)S(1)} %bitcast.37), kind=kOutput, calls=%fused_computation.2 | convolution fusion | flops 8543232000 | bytes 72990728 | tf_op jit(solution)/shard_map/irk,irl->ikl/dot_general | solution.py:53
  424.8 564.5 %reduce_scatter.22 = f32[360,11520]{1,0:T(8,128)} reduce-scatter(f32[1440,11520]{1,0:T(8,128)} %multiply_reduce_fusion), channel_id=1, replica_groups=mesh['client'=4,'blk'=8] {'client'}, use_global_device_ids=true, dimensions={0}, to_apply=%region_1.2 | reduce-scatter | bytes 82944000 | tf_op jit(solution)/shard_map/reduce_scatter | solution.py:58
  989.2 11.7 %multiply_select_fusion = f32[360,11520]{1,0:T(8,128)} fusion(f32[360,11520]{1,0:T(8,128)} %reduce_scatter.22, s32[360]{0:T(512)S(1)} %iota_add_fusion), kind=kLoop, calls=%fused_computation.3 | loop fusion | flops 12441600 | bytes 33179040 | tf_op jit(solution)/shard_map/jit(_where)/select_n | solution.py:67
  1000.9 0.0 reduce-scatter.3.cloned.1.call-done
  (14 shorter events, 0.4 us)
Async XLA Ops:
  12.6 14.3 %all-to-all-start = ((bf16[8,2,2560]{2,1,0:T(2,128)(2,1)}), bf16[8,2,2560]{2,1,0:T(2,128)(2,1)S(1)}, u32[]{:S(2)}, u32[]{:S(2)}) async-start(bf16[8,2,2560]{2,1,0:T(2,128)(2,1)} %reshape.72), calls=%async_computation | async-start | bytes 163840 | tf_op jit(solution)/shard_map/all_to_all | solution.py:38
  19.9 981.0 %reduce-scatter.3.cloned.1.call-start = ((), (), s32[]{:S(2)}) async-start(), calls=%async_computation.3 | async-start | bytes 9216000 | tf_op jit(solution)/shard_map/reduce_scatter | solution.py:59
  30.5 3.8 copy-start.1
  132.3 0.8 copy-start.3
  132.3 0.9 copy-start.2
  331.1 2.6 copy-start
Sparse Core Ops, SparseCore 0:
  132.4 64.4 reduce-scatter.2
where the time goes:
time: 1010 us
  blocking collectives  827 us (82%)
  local copies, waits for them, and re-layouts  78.9 us (8%)
  matrix products  57 us (6%)
  other arithmetic  16.7 us (2%)
  between operations  14.4 us (1%)
    reduce_scatter x1, blocking collectives, body(): lax.psum_scatter(gram_rows, 'client', scatter_dimension=0, tiled=True)  564 us
    all_gather x1, blocking collectives, body(): their_patch = patch_rows(lax.all_gather(tiles, 'blk', axis=4, tiled=True))  186 us
    psum x1, blocking collectives, body(): summed_out = lax.psum(partial_out, 'blk')  76.6 us
    dot_general x1, matrix products, body(): jnp.einsum('irk,irl->ikl', own_patch, their_patch, preferred_element_type...  43.8 us
    gather x2, local copies, waits for them, and re-layouts, patch_rows(): return jnp.take(joined, jnp.asarray(column_order), axis=2)  37 us
  transfers between devices with their start and end apart: 2, of which 1 were waited for; matrix products, arithmetic and copies ran while one was open for 11% of the time, Pallas kernels for 0%

commit v1 on v0

v1 whole, which is shorter than its diff:
```python
import functools

import jax
import jax.numpy as jnp
from jax import lax
from jax.experimental import pallas as pl
from jax.experimental.pallas import tpu as pltpu
from jax.sharding import PartitionSpec as P

keep_off = 0.9
LANES = 128


def expand(x_ref, scratch, height, width):
    channels, pixels = x_ref.shape
    lane = lax.broadcasted_iota(jnp.int32, (1, pixels), 1)
    col = lane % width
    row = (lane // width) % height

    def shifted(value, step, inside):
        return jnp.where(inside, pltpu.roll(value, (-step) % pixels, 1), 0.0)

    for first in range(0, channels, 16):
        size = min(16, channels - first)
        base = x_ref[first : first + size, :].astype(jnp.float32)
        for b in range(3):
            if b == 1:
                across = base
            else:
                across = shifted(base, b - 1, (col + (b - 1) >= 0) & (col + (b - 1) < width))
            for a in range(3):
                if a == 1:
                    both = across
                else:
                    both = shifted(across, (a - 1) * width, (row + (a - 1) >= 0) & (row + (a - 1) < height))
                for chunk in range(pixels // LANES):
                    scratch[chunk, pl.ds(first * 9 + 3 * a + b, size, stride=9), :] = both[
                        :, chunk * LANES : (chunk + 1) * LANES
                    ]


def gram_kernel(height, width, first_ref, x_ref, own_ref, scale_ref, gram_ref, mine_ref, wide, narrow, mine_wide):
    step = pl.program_id(0)
    chunks = wide.shape[0]

    @pl.when(step == 0)
    def _():
        expand(own_ref, mine_wide, height, width)
        for chunk in range(chunks):
            part = slice(chunk * LANES, (chunk + 1) * LANES)
            mine_ref[:, part] = (mine_wide[chunk] * scale_ref[:, part]).astype(jnp.bfloat16)

    expand(x_ref, wide, height, width)
    for chunk in range(chunks):
        narrow[:, chunk * LANES : (chunk + 1) * LANES] = wide[chunk].astype(jnp.bfloat16)
    product = lax.dot_general(
        mine_ref[...], narrow[...], (((1,), (1,)), ((), ())), preferred_element_type=jnp.float32
    )
    where_diag = first_ref[0] - step * product.shape[1]
    on_diag = (
        lax.broadcasted_iota(jnp.int32, product.shape, 1)
        == lax.broadcasted_iota(jnp.int32, product.shape, 0) + where_diag
    )
    gram_ref[...] = jnp.where(on_diag, product, keep_off * product)


def gram_call(first_row, xt, own, scale_row, height, width):
    channels, pixels = xt.shape
    mine = own.shape[0]
    tile = LANES
    return pl.pallas_call(
        functools.partial(gram_kernel, height, width),
        grid=(channels // tile,),
        in_specs=[
            pl.BlockSpec(memory_space=pltpu.SMEM),
            pl.BlockSpec((tile, pixels), lambda j: (j, 0)),
            pl.BlockSpec((mine, pixels), lambda j: (0, 0)),
            pl.BlockSpec((1, pixels), lambda j: (0, 0)),
        ],
        out_specs=[
            pl.BlockSpec((mine * 9, tile * 9), lambda j: (0, j)),
            pl.BlockSpec((mine * 9, pixels), lambda j: (0, 0)),
        ],
        out_shape=[
            jax.ShapeDtypeStruct((mine * 9, channels * 9), jnp.float32),
            jax.ShapeDtypeStruct((mine * 9, pixels), jnp.bfloat16),
        ],
        scratch_shapes=[
            pltpu.VMEM((pixels // LANES, tile * 9, LANES), jnp.float32),
            pltpu.VMEM((tile * 9, pixels), jnp.bfloat16),
            pltpu.VMEM((pixels // LANES, mine * 9, LANES), jnp.float32),
        ],
        compiler_params=pltpu.CompilerParams(vmem_limit_bytes=60 * 1024 * 1024),
        cost_estimate=pl.CostEstimate(
            flops=2 * mine * 9 * channels * 9 * pixels,
            bytes_accessed=mine * channels * 81 * 4,
            transcendentals=0,
        ),
    )(first_row, xt, own, scale_row)


def local_kernel(height, width, x_ref, scale_ref, w_ref, out_ref, damp_ref, wide):
    group = pl.program_id(1)
    expand(x_ref.at[0], wide, height, width)
    weights = w_ref[0]
    square = jnp.zeros((wide.shape[1], 1), jnp.float32)
    for chunk in range(wide.shape[0]):
        patch = wide[chunk]
        square += jnp.sum(patch * patch, axis=1, keepdims=True)
        out_ref[0, chunk * LANES : (chunk + 1) * LANES, :] = lax.dot_general(
            patch.astype(jnp.bfloat16), weights, (((0,), (0,)), ((), ())), preferred_element_type=jnp.float32
        )
    term = (square * (scale_ref[group] * (1.0 - keep_off))) * weights.astype(jnp.float32)

    @pl.when(group == 0)
    def _():
        damp_ref[...] = term

    @pl.when(group > 0)
    def _():
        damp_ref[...] += term


def local_call(x_own, my_scale, weights, height, width):
    groups, channels, pixels = x_own.shape
    rows, columns = weights.shape[1:]
    half = columns // 2
    return pl.pallas_call(
        functools.partial(local_kernel, height, width),
        grid=(2, groups),
        in_specs=[
            pl.BlockSpec((1, channels, pixels), lambda n, i: (i, 0, 0)),
            pl.BlockSpec(memory_space=pltpu.SMEM),
            pl.BlockSpec((1, rows, half), lambda n, i: (i, 0, n)),
        ],
        out_specs=[
            pl.BlockSpec((1, pixels, half), lambda n, i: (i, 0, n)),
            pl.BlockSpec((rows, half), lambda n, i: (0, n)),
        ],
        out_shape=[
            jax.ShapeDtypeStruct((groups, pixels, columns), jnp.float32),
            jax.ShapeDtypeStruct((rows, columns), jnp.float32),
        ],
        scratch_shapes=[pltpu.VMEM((pixels // LANES, rows, LANES), jnp.float32)],
        compiler_params=pltpu.CompilerParams(vmem_limit_bytes=60 * 1024 * 1024),
        cost_estimate=pl.CostEstimate(
            flops=2 * groups * pixels * rows * columns,
            bytes_accessed=groups * rows * columns * 2,
            transcendentals=0,
        ),
    )(x_own, my_scale, weights)


def body(activations, sample_count, client_weights):
    blk_count = lax.axis_size("blk")
    client_here = lax.axis_index("client")
    blk_here = lax.axis_index("blk")
    group_size, slot_count, rows_here, width, channels = activations.shape
    height = rows_here * blk_count
    client_total = sample_count.shape[0]
    client_groups = client_total // group_size
    image = slot_count * height * width
    scale = 1.0 / (client_total * sample_count.astype(jnp.float32) * (height * width))
    live = lax.broadcasted_iota(jnp.int32, (client_total, slot_count), 1) < sample_count[:, None]

    gathered = lax.all_gather(activations, ("client", "blk"), axis=0, tiled=False)
    gathered = gathered.reshape(
        client_groups, blk_count, group_size, slot_count, rows_here, width, channels
    )
    xt = gathered.transpose(6, 0, 2, 3, 1, 4, 5).reshape(channels, client_total, slot_count, height * width)
    xt = jnp.where(live[None, :, :, None], xt, jnp.zeros_like(xt)).reshape(channels, client_total * image)

    tile = channels // blk_count
    mine = tile // client_groups
    tile_x = lax.dynamic_slice_in_dim(xt, blk_here * tile, tile, 0)
    own_x = lax.dynamic_slice_in_dim(tile_x, client_here * mine, mine, 0)
    group_x = lax.dynamic_slice_in_dim(tile_x, client_here * group_size * image, group_size * image, 1)
    group_x = group_x.reshape(tile, group_size, image).transpose(1, 0, 2)
    my_scale = lax.dynamic_slice_in_dim(scale, client_here * group_size, group_size)

    partial_out, damp = local_call(group_x, my_scale, client_weights, height, width)
    partial_out = partial_out.reshape(group_size * image, -1)
    out_share = lax.psum_scatter(partial_out, "blk", scatter_dimension=0, tiled=True)
    outs = lax.all_gather(out_share.astype(jnp.bfloat16), ("client", "blk"), axis=0, tiled=True)
    damp_mine = lax.psum_scatter(damp.astype(jnp.bfloat16), "client", scatter_dimension=0, tiled=True)

    first_row = (blk_here * tile + client_here * mine) * 9
    scale_row = jnp.repeat(scale, image)[None, :]
    gram, scaled = gram_call(
        first_row.astype(jnp.int32)[None], xt, own_x, scale_row, height, width
    )
    cross = jnp.dot(scaled, outs, preferred_element_type=jnp.float32)
    return gram, keep_off * cross + damp_mine.astype(jnp.float32)


def solution(mesh):
    in_specs = (P("client", None, "blk", None, None), P(), P("client", "blk", None))
    out_specs = (P(("blk", "client"), None), P(("blk", "client"), None))
    return jax.shard_map(body, mesh=mesh, in_specs=in_specs, out_specs=out_specs, check_vma=False)
```

time: 1010 us -> 270 us (0.27)
  blocking collectives: 827 us -> 0 us
  waiting for transfers between devices: 6.28 us -> 194 us
  local copies, waits for them, and re-layouts: 78.9 us -> 11.8 us
  matrix products: 57 us -> 4.55 us
  Pallas kernels: 0 us -> 37 us
    reduce_scatter x1 -> x0, blocking collectives: 564 us -> none  [body(): lax.psum_scatter(gram_rows, 'client', scatter_dimension=0, tiled=True)]
    all_gather x1 -> x0, blocking collectives: 186 us -> none  [body(): their_patch = patch_rows(lax.all_gather(tiles, 'blk', axis=4, tiled=True))]
    all_gather x0 -> x2, waiting for transfers between devices: none -> 122 us  [the longest x1 61.3 us: body(): lax.all_gather(activations, ('client', 'blk'), axis=0, tiled=False)]
    psum x1 -> x0, blocking collectives: 76.6 us -> none  [body(): summed_out = lax.psum(partial_out, 'blk')]
    reduce_scatter x1 -> x2, waiting for transfers between devices: 0.01 us -> 71.2 us  [the longest x1 58.6 us: body(): lax.psum_scatter(partial_out, 'blk', scatter_dimension=0, tiled=True)]
    dot_general x3 -> x1, matrix products: 57 us -> 4.55 us  [body(): cross = jnp.dot(scaled, outs, preferred_element_type=jnp.float32)]
    gather x2 -> x0, local copies, waits for them, and re-layouts: 37 us -> none  [patch_rows(): return jnp.take(joined, jnp.asarray(column_order), axis=2)]
    pallas_call x0 -> x2, Pallas kernels: none -> 37 us  [the longest x1 26.4 us: gram_call(): pl.pallas_call(functools.partial(gram_kernel, height, width), grid=(chann...]
  transfers between devices with their start and end apart: 2 -> 4, of which waited for: 1 -> 4; matrix products, arithmetic and copies ran while one was open for 11% -> 4% of each run, Pallas kernels for 0% -> 10%
where the time goes in v1:
time: 270 us; the launch traced here: 269 us
  waiting for transfers between devices  194 us (72%)
  Pallas kernels  37 us (14%)
  between operations  13.8 us (5%)
  local copies, waits for them, and re-layouts  11.8 us (4%)
  other arithmetic  8.38 us (3%)
  matrix products  4.55 us (2%)
    all_gather x1, waiting for transfers between devices, body(): lax.all_gather(activations, ('client', 'blk'), axis=0, tiled=False)  61.3 us
    all_gather x1, waiting for transfers between devices, body(): lax.all_gather(out_share.astype(jnp.bfloat16), ('client', 'blk'), axis=0,...  60.6 us
    reduce_scatter x1, waiting for transfers between devices, body(): lax.psum_scatter(partial_out, 'blk', scatter_dimension=0, tiled=True)  58.6 us
    pallas_call x1, Pallas kernels, gram_call(): pl.pallas_call(functools.partial(gram_kernel, height, width), grid=(chann...  26.4 us
    reduce_scatter x1, waiting for transfers between devices, body(): lax.psum_scatter(damp.astype(jnp.bfloat16), 'client', scatter_dimension=0...  12.6 us
    pallas_call x1, Pallas kernels, local_call(): pl.pallas_call(functools.partial(local_kernel, height, width), grid=(2, g...  10.6 us
  transfers between devices with their start and end apart: 4, of which 4 were waited for; matrix products, arithmetic and copies ran while one was open for 4% of the time, Pallas kernels for 10%

profile of v1, /device:TPU:0, one launch (start us, length us, event | category | flops | bytes accessed | tf_op | source)
XLA Modules:
  0.0 269.5 jit_solution(15964011859836346675)
XLA Ops:
  7.2 0.0 all-gather.6.cloned.1.call-start
  7.2 0.7 all-gather.6.cloned.1.call-update
  7.9 0.0 reduce-scatter.3.cloned.1.call-start
  8.0 0.7 iota_compare_fusion
  8.7 0.1 broadcast_in_dim.24
  8.8 0.1 broadcast_in_dim.25
  8.8 0.7 multiply_divide_fusion
  9.5 0.7 dynamic_slice.15.scale_ref
  10.2 61.3 %all-gather.6.cloned.1.call-done = bf16[64,2,1,8,1280]{4,3,2,1,0:T(8,128)(2,1)} async-done(((bf16[2,2,1,8,1280]{4,3,2,1,0:T(8,128)(2,1)}), bf16[64,2,1,8,1280]{4,3,2,1,0:T(8,128)(2,1)}) %all-gather.6.cloned.1.call-update) | async-done | bytes 2621456 | tf_op jit(solution)/shard_map/all_gather | solution.py:166
  71.4 3.5 %copy.12 = bf16[1280,4,2,2,8,1,8]{0,6,4,3,2,1,5:T(8,128)(2,1)} copy(bf16[1280,4,2,2,8,1,8]{0,6,3,2,4,1,5:T(8,128)(2,1)} %bitcast.17) | data formatting | bytes 5242880 | tf_op jit(solution)/shard_map/transpose | solution.py:170
  75.0 3.0 %copy.13 = bf16[1280,1024]{1,0:T(8,128)(2,1)S(1)} copy(bf16[1280,1024]{0,1:T(8,128)(2,1)} %bitcast.16) | data formatting | bytes 5242880 | tf_op jit(solution)/shard_map/reshape | solution.py:170
  78.0 0.2 broadcast_select_fusion.x_ref
  78.1 0.0 copy-start
  78.2 1.5 copy-done
  79.6 0.7 bitcast_bitcast_fusion.x_ref
  80.4 10.6 %shard_map.51 = (f32[2,128,1280]{2,1,0:T(8,128)}, f32[1440,1280]{1,0:T(8,128)}) custom-call(bf16[2,160,128]{2,1,0:T(8,128)(2,1)} %bitcast_bitcast_fusion.x_ref, f32[2]{0:T(128)} %dynamic_slice.15.scale_ref, bf16[2,1440,1280]{2,1,0:T(8,128)(2,1)} %w_ref.1), custom_call_target="tpu_custom_call" | custom-call | flops 943718400 | bytes 7372800 | tf_op jit(solution)/shard_map/pallas_call | solution.py:128
  90.9 0.0 reduce-scatter.3.cloned.1.call-update
  91.0 0.0 reduce-scatter.5.cloned.1.call-start
  91.0 5.3 %convert_element_type.14 = bf16[1440,1280]{1,0:T(8,128)(2,1)} convert(f32[1440,1280]{1,0:T(8,128)} %get-tuple-element.9) | non-fusion elementwise | flops 1843200 | bytes 11059200 | tf_op jit(solution)/shard_map/convert_element_type | solution.py:185
  96.3 0.0 reduce-scatter.5.cloned.1.call-update
  96.3 0.0 all-gather.4.cloned.1.call-start
  96.3 58.6 %reduce-scatter.3.cloned.1.call-done = f32[32,1280]{1,0:T(8,128)} async-done(((f32[256,1280]{1,0:T(8,128)}), f32[32,1280]{1,0:T(8,128)}) %reduce-scatter.3.cloned.1.call-update) | async-done | bytes 163856 | tf_op jit(solution)/shard_map/reduce_scatter | solution.py:183
  154.9 1.6 convert_element_type.13
  156.5 0.0 all-gather.4.cloned.1.call-update
  156.5 1.6 constant_dynamic-slice_fusion.own_ref
  158.1 0.7 broadcast_in_dim.28
  158.7 26.4 %shard_map.50 = (f32[360,11520]{1,0:T(8,128)}, bf16[360,1024]{1,0:T(8,128)(2,1)}) custom-call(s32[1]{0:T(128)} %bitcast.first_ref, bf16[1280,1024]{1,0:T(8,128)(2,1)} %copy-done, bf16[40,1024]{1,0:T(8,128)(2,1)} %constant_dynamic-slice_fusion.own_ref, f32[1,1024]{1,0:T(1,128)} %bitcast.19), custom_call_target="tpu_custom_call" | custom-call | flops 8493465600 | bytes 16588800 | tf_op jit(solution)/shard_map/pallas_call | solution.py:71
  185.2 12.6 %reduce-scatter.5.cloned.1.call-done = bf16[360,1280]{1,0:T(8,128)(2,1)} async-done(((bf16[1440,1280]{1,0:T(8,128)(2,1)}), bf16[360,1280]{1,0:T(8,128)(2,1)}) %reduce-scatter.5.cloned.1.call-update) | async-done | bytes 921616 | tf_op jit(solution)/shard_map/reduce_scatter | solution.py:185
  197.8 60.6 %all-gather.4.cloned.1.call-done = bf16[1024,1280]{1,0:T(8,128)(2,1)} async-done(((bf16[32,1280]{1,0:T(8,128)(2,1)}), bf16[1024,1280]{1,0:T(8,128)(2,1)}) %all-gather.4.cloned.1.call-update) | async-done | bytes 2621456 | tf_op jit(solution)/shard_map/all_gather | solution.py:184
  258.4 4.6 %fusion = f32[360,1280]{1,0:T(8,128)} fusion(bf16[360,1024]{1,0:T(8,128)(2,1)} %get-tuple-element.7, bf16[1024,1280]{1,0:T(8,128)(2,1)} %all-gather.4.cloned.1.call-done, bf16[360,1280]{1,0:T(8,128)(2,1)} %reduce-scatter.5.cloned.1.call-done), kind=kOutput, calls=%fused_computation.1 | convolution fusion | flops 945100800 | bytes 6123520 | tf_op jit(solution)/shard_map/dot_general | solution.py:192
Async XLA Ops:
  7.2 64.3 %all-gather.6.cloned.1.call-start = ((), (), s32[]{:S(2)}) async-start(), calls=%async_computation.5 | async-start | bytes 2703360 | tf_op jit(solution)/shard_map/all_gather | solution.py:166
  7.9 147.0 %reduce-scatter.3.cloned.1.call-start = ((), (), s32[]{:S(2)}) async-start(), calls=%async_computation.2 | async-start | bytes 1474560 | tf_op jit(solution)/shard_map/reduce_scatter | solution.py:183
  78.1 1.5 copy-start
  91.0 106.8 %reduce-scatter.5.cloned.1.call-start = ((), (), s32[]{:S(2)}) async-start(), calls=%async_computation.4 | async-start | bytes 4608000 | tf_op jit(solution)/shard_map/reduce_scatter | solution.py:185
  96.3 162.1 %all-gather.4.cloned.1.call-start = ((), (), s32[]{:S(2)}) async-start(), calls=%async_computation.3 | async-start | bytes 2703360 | tf_op jit(solution)/shard_map/all_gather | solution.py:184
Sparse Core Ops, SparseCore 0:
  10.9 60.5 all-gather.5
  91.1 63.7 reduce-scatter.2
  157.5 40.2 reduce-scatter.4
  200.6 57.7 all-gather.3

commit v2 on v1

v2 whole, which is shorter than its diff:
```python
import functools

import jax
import jax.numpy as jnp
from jax import lax
from jax.experimental import pallas as pl
from jax.experimental.pallas import tpu as pltpu
from jax.sharding import PartitionSpec as P

keep_off = 0.9
LANES = 128


MESH = pl.DeviceIdType.MESH


def expand(base_of, live, channels, scratch, height, stride, width):
    pixels = live.shape[1]
    lane = lax.broadcasted_iota(jnp.int32, (1, pixels), 1)
    col = lane % width
    row = (lane // stride) % height

    def shifted(value, step, inside):
        return jnp.where(inside, pltpu.roll(value, (-step) % pixels, 1), 0.0)

    for first in range(0, channels, 16):
        size = min(16, channels - first)
        base = jnp.where(live > 0.0, base_of(first, size), 0.0)
        for b in range(3):
            if b == 1:
                across = base
            else:
                across = shifted(base, b - 1, (col + (b - 1) >= 0) & (col + (b - 1) < width))
            for a in range(3):
                if a == 1:
                    both = across
                else:
                    both = shifted(across, (a - 1) * stride, (row + (a - 1) >= 0) & (row + (a - 1) < height))
                for chunk in range(pixels // LANES):
                    scratch[chunk, pl.ds(first * 9 + 3 * a + b, size, stride=9), :] = both[
                        :, chunk * LANES : (chunk + 1) * LANES
                    ]


def gather_kernel(x_ref, out_ref, recv_sem, send_sem):
    clients, blks = out_ref.shape[:2]
    rows = out_ref.shape[2]
    depth = blks // 2
    client, blk = lax.axis_index("client"), lax.axis_index("blk")
    core_mate = client + 1 - 2 * (client % 2)
    x_mate = (client + 2) % clients
    z, y = blk // 2, blk % 2
    y_mate = blk + 1 - 2 * y
    core_dev, x_dev, y_dev = (core_mate, blk), (x_mate, blk), (client, y_mate)
    up_dev, down_dev = (client, blk + 2), (client, blk - 2)
    half = rows // 2

    barrier = pltpu.get_barrier_semaphore()
    for device in (core_dev, x_dev, y_dev):
        pl.semaphore_signal(barrier, inc=1, device_id=device, device_id_type=MESH)

    @pl.when(z + 1 < depth)
    def _():
        pl.semaphore_signal(barrier, inc=1, device_id=up_dev, device_id_type=MESH)

    @pl.when(z > 0)
    def _():
        pl.semaphore_signal(barrier, inc=1, device_id=down_dev, device_id_type=MESH)

    pl.semaphore_wait(barrier, 3 + jnp.where(z > 0, 1, 0) + jnp.where(z + 1 < depth, 1, 0))

    def copy(lane, c, b, device, part=None, own=False):
        where = (c, b) if part is None else (c, b, pl.ds(part * half, half))
        dst = out_ref.at[where]
        src = dst
        if own:
            src = x_ref
        if part is None:
            recv = recv_sem.at[0, c * blks + b]
        else:
            recv = recv_sem.at[part, c * blks + b]
        return pltpu.make_async_remote_copy(
            src_ref=src,
            dst_ref=dst,
            send_sem=send_sem.at[lane, c * blks + b],
            recv_sem=recv,
            device_id=device,
            device_id_type=MESH,
        )

    def along_z(offset):
        if offset == 0:
            return None
        level = z + offset
        return (level >= 0) & (level < depth)

    def guarded(offset, action):
        inside = along_z(offset)
        if inside is None:
            action(blk)
        else:
            pl.when(inside)(lambda: action(blk + 2 * offset))

    order = [0]
    for distance in range(1, depth):
        order += [-distance, distance]

    for offset in order:

        def first(b):
            own = offset == 0
            if not own:
                copy(0, client, b, core_dev).wait_recv()
            if offset <= 0:

                @pl.when(z + 1 < depth)
                def _():
                    copy(0, client, b, up_dev, own=own).start()

            if offset >= 0:

                @pl.when(z > 0)
                def _():
                    copy(1, client, b, down_dev, own=own).start()

            copy(2, client, b, x_dev, own=own).start()
            copy(3, client, b, y_dev, own=own).start()
            copy(4, client, b, core_dev, own=own).start()

        guarded(offset, first)

    def mate_of(b):
        return b + 1 - 2 * y

    for offset in order:

        def second(b):
            copy(0, x_mate, b, core_dev).wait_recv()
            copy(3, x_mate, b, y_dev, part=0).start()
            copy(4, x_mate, b, core_dev).start()
            copy(0, client, mate_of(b), core_dev).wait_recv()
            copy(2, client, mate_of(b), x_dev, part=1).start()
            copy(4, client, mate_of(b), core_dev).start()

        guarded(offset, second)

    for offset in order:

        def third(b):
            copy(0, x_mate, mate_of(b), core_dev, part=0).wait_recv()
            copy(0, x_mate, mate_of(b), core_dev, part=1).wait_recv()
            copy(4, x_mate, mate_of(b), core_dev).start()

        guarded(offset, third)

    for offset in order:

        def fourth(b):
            far = (core_mate + 2) % clients
            for c, bb in ((core_mate, b), (far, b), (core_mate, mate_of(b)), (far, mate_of(b))):
                copy(0, c, bb, core_dev).wait_recv()
            own = offset == 0
            if offset <= 0:

                @pl.when(z + 1 < depth)
                def _():
                    copy(0, client, b, up_dev, own=own).wait_send()

            if offset >= 0:

                @pl.when(z > 0)
                def _():
                    copy(1, client, b, down_dev, own=own).wait_send()

            copy(2, client, b, x_dev, own=own).wait_send()
            copy(3, client, b, y_dev, own=own).wait_send()
            copy(4, client, b, core_dev, own=own).wait_send()
            copy(3, x_mate, b, y_dev, part=0).wait_send()
            copy(4, x_mate, b, core_dev).wait_send()
            copy(2, client, mate_of(b), x_dev, part=1).wait_send()
            copy(4, client, mate_of(b), core_dev).wait_send()
            copy(4, x_mate, mate_of(b), core_dev).wait_send()

        guarded(offset, fourth)

    out_ref[client, blk] = x_ref[...]


def gather_call(x, clients, blks):
    return pl.pallas_call(
        gather_kernel,
        in_specs=[pl.BlockSpec(memory_space=pltpu.VMEM)],
        out_specs=pl.BlockSpec(memory_space=pltpu.VMEM),
        out_shape=jax.ShapeDtypeStruct((clients, blks) + x.shape, x.dtype),
        scratch_shapes=[
            pltpu.SemaphoreType.DMA((2, clients * blks)),
            pltpu.SemaphoreType.DMA((5, clients * blks)),
        ],
        compiler_params=pltpu.CompilerParams(
            collective_id=1, has_side_effects=True, vmem_limit_bytes=40 * 1024 * 1024
        ),
    )(x)


def reduce_kernel(part_ref, out_ref, ybuf, sums, zbuf, ys, yr, zs, zr, gs, gr, fs, fr):
    pieces, depth = part_ref.shape[:2]
    client, blk = lax.axis_index("client"), lax.axis_index("blk")
    z, y = blk // 2, blk % 2
    other = 1 - y
    y_dev = (client, blk + 1 - 2 * y)

    def level(d):
        return (z + d) % depth

    def z_dev(d):
        return (client, level(d) * 2 + y)

    barrier = pltpu.get_barrier_semaphore()
    pl.semaphore_signal(barrier, inc=1, device_id=y_dev, device_id_type=MESH)
    for d in range(1, depth):
        pl.semaphore_signal(barrier, inc=1, device_id=z_dev(d), device_id_type=MESH)
    pl.semaphore_wait(barrier, depth)

    def send(src, dst, send_sem, recv_sem, device):
        return pltpu.make_async_remote_copy(
            src_ref=src, dst_ref=dst, send_sem=send_sem, recv_sem=recv_sem, device_id=device, device_id_type=MESH
        )

    def y_copy(q):
        return send(part_ref.at[q, :, other], ybuf.at[q], ys.at[q], yr.at[q], y_dev)

    def z_copy(q, d):
        return send(sums.at[q, level(d)], zbuf.at[q, d], zs.at[q, d], zr.at[q, d], z_dev(d))

    def share(q, d, to):
        here = out_ref.at[q, level(d), y]
        return send(here, here, gs.at[q, to], gr.at[q, to], z_dev(to))

    def forward(q, d, column):
        here = out_ref.at[q, level(d), column]
        return send(here, here, fs.at[q, d], fr.at[q, level(d)], y_dev)

    for q in range(pieces):
        y_copy(q).start()

    def add_y(q):
        y_copy(q).wait_recv()
        for d in range(depth):
            sums[q, level(d)] = part_ref[q, level(d), y] + ybuf[q, level(d)]
        for d in range(1, depth):
            z_copy(q, d).start()

    def add_z(q):
        total = sums[q, z]
        for d in range(1, depth):
            z_copy(q, d).wait_recv()
            total = total + zbuf[q, d]
        out_ref[q, z, y] = total.astype(jnp.bfloat16)
        for d in range(1, depth):
            share(q, 0, d).start()
        forward(q, 0, y).start()

    def pass_on(q):
        for d in range(1, depth):
            share(q, depth - d, d).wait_recv()
            forward(q, depth - d, y).start()

    for step in range(pieces + 2):
        if step < pieces:
            add_y(step)
        if 0 <= step - 1 < pieces:
            add_z(step - 1)
        if 0 <= step - 2 < pieces:
            pass_on(step - 2)

    for q in range(pieces):
        y_copy(q).wait_send()
        for d in range(1, depth):
            z_copy(q, d).wait_send()
            share(q, 0, d).wait_send()
        for d in range(depth):
            forward(q, d, y).wait_send()
            forward(q, d, other).wait_recv()


def reduce_call(partial):
    pieces, depth, two, rows, columns = partial.shape
    sem = pltpu.SemaphoreType.DMA
    return pl.pallas_call(
        reduce_kernel,
        in_specs=[pl.BlockSpec(memory_space=pltpu.VMEM)],
        out_specs=pl.BlockSpec(memory_space=pltpu.VMEM),
        out_shape=jax.ShapeDtypeStruct(partial.shape, jnp.bfloat16),
        scratch_shapes=[
            pltpu.VMEM((pieces, depth, rows, columns), jnp.float32),
            pltpu.VMEM((pieces, depth, rows, columns), jnp.float32),
            pltpu.VMEM((pieces, depth, rows, columns), jnp.float32),
            sem((pieces,)),
            sem((pieces,)),
            sem((pieces, depth)),
            sem((pieces, depth)),
            sem((pieces, depth)),
            sem((pieces, depth)),
            sem((pieces, depth)),
            sem((pieces, depth)),
        ],
        compiler_params=pltpu.CompilerParams(
            collective_id=2, has_side_effects=True, vmem_limit_bytes=50 * 1024 * 1024
        ),
    )(partial)


def gram_kernel(height, stride, width, first_ref, x_ref, own_ref, scale_ref, live_ref, gram_ref, wide, narrow, mine_wide, mine_ref, flipped):
    step = pl.program_id(0)
    chunks = wide.shape[0]

    live = live_ref[...]

    @pl.when(step == 0)
    def _():
        expand(
            lambda first, size: own_ref[first : first + size, :].astype(jnp.float32),
            live, own_ref.shape[0], mine_wide, height, stride, width,
        )
        for chunk in range(chunks):
            part = slice(chunk * LANES, (chunk + 1) * LANES)
            mine_ref[:, part] = (mine_wide[chunk] * scale_ref[:, part]).astype(jnp.bfloat16)

    flipped[...] = x_ref[...].astype(jnp.float32).T
    expand(
        lambda first, size: flipped[first : first + size, :],
        live, flipped.shape[0], wide, height, stride, width,
    )
    for chunk in range(chunks):
        narrow[:, chunk * LANES : (chunk + 1) * LANES] = wide[chunk].astype(jnp.bfloat16)
    product = lax.dot_general(
        mine_ref[...], narrow[...], (((1,), (1,)), ((), ())), preferred_element_type=jnp.float32
    )
    where_diag = first_ref[0] - step * product.shape[1]
    on_diag = (
        lax.broadcasted_iota(jnp.int32, product.shape, 1)
        == lax.broadcasted_iota(jnp.int32, product.shape, 0) + where_diag
    )
    gram_ref[...] = jnp.where(on_diag, product, keep_off * product)


def gram_call(first_row, x, own, scale_row, live_row, height, stride, width):
    pixels, channels = x.shape
    mine = own.shape[0]
    tile = LANES
    return pl.pallas_call(
        functools.partial(gram_kernel, height, stride, width),
        grid=(channels // tile,),
        in_specs=[
            pl.BlockSpec(memory_space=pltpu.SMEM),
            pl.BlockSpec((pixels, tile), lambda j: (0, j)),
            pl.BlockSpec((mine, pixels), lambda j: (0, 0)),
            pl.BlockSpec((1, pixels), lambda j: (0, 0)),
            pl.BlockSpec((1, pixels), lambda j: (0, 0)),
        ],
        out_specs=pl.BlockSpec((mine * 9, tile * 9), lambda j: (0, j)),
        out_shape=jax.ShapeDtypeStruct((mine * 9, channels * 9), jnp.float32),
        scratch_shapes=[
            pltpu.VMEM((pixels // LANES, tile * 9, LANES), jnp.float32),
            pltpu.VMEM((tile * 9, pixels), jnp.bfloat16),
            pltpu.VMEM((pixels // LANES, mine * 9, LANES), jnp.float32),
            pltpu.VMEM((mine * 9, pixels), jnp.bfloat16),
            pltpu.VMEM((tile, pixels), jnp.float32),
        ],
        compiler_params=pltpu.CompilerParams(vmem_limit_bytes=60 * 1024 * 1024),
        cost_estimate=pl.CostEstimate(
            flops=2 * mine * 9 * channels * 9 * pixels,
            bytes_accessed=mine * channels * 81 * 4,
            transcendentals=0,
        ),
    )(first_row, x, own, scale_row, live_row)


def local_kernel(height, stride, width, x_ref, live_ref, who_ref, scale_ref, w_ref, out_ref, damp_ref, patch_ref, wide, square):
    piece = pl.program_id(0)
    groups = w_ref.shape[0]
    chunks = wide.shape[0]
    who = who_ref[...]

    @pl.when(piece == 0)
    def _():
        expand(
            lambda first, size: x_ref[first : first + size, :].astype(jnp.float32),
            live_ref[...], x_ref.shape[0], wide, height, stride, width,
        )
        for group in range(groups):
            sums = jnp.zeros((wide.shape[1], 1), jnp.float32)
            for chunk in range(chunks):
                part = slice(chunk * LANES, (chunk + 1) * LANES)
                patch = wide[chunk]
                sums += jnp.sum(jnp.where(who[:, part] == group, patch * patch, 0.0), axis=1, keepdims=True)
                patch_ref[:, part] = patch.astype(jnp.bfloat16)
            square[group] = sums * (scale_ref[group] * (1.0 - keep_off))

    patches = patch_ref[...]
    total = None
    damp = None
    for group in range(groups):
        weights = w_ref[group]
        picked = jnp.where(who == group, patches, jnp.zeros_like(patches))
        term = lax.dot_general(picked, weights, (((0,), (0,)), ((), ())), preferred_element_type=jnp.float32)
        scaled = square[group] * weights.astype(jnp.float32)
        total = term if total is None else total + term
        damp = scaled if damp is None else damp + scaled
    out_ref[0] = total
    damp_ref[0] = damp


def local_call(x, live, who, my_scale, weights, pieces, height, stride, width):
    channels, pixels = x.shape
    groups, rows, columns = weights.shape
    wide = columns // pieces
    return pl.pallas_call(
        functools.partial(local_kernel, height, stride, width),
        grid=(pieces,),
        in_specs=[
            pl.BlockSpec((channels, pixels), lambda n: (0, 0)),
            pl.BlockSpec((1, pixels), lambda n: (0, 0)),
            pl.BlockSpec((1, pixels), lambda n: (0, 0)),
            pl.BlockSpec(memory_space=pltpu.SMEM),
            pl.BlockSpec((groups, rows, wide), lambda n: (0, 0, n)),
        ],
        out_specs=[
            pl.BlockSpec((1, pixels, wide), lambda n: (n, 0, 0)),
            pl.BlockSpec((1, rows, wide), lambda n: (n, 0, 0)),
            pl.BlockSpec((rows, pixels), lambda n: (0, 0)),
        ],
        out_shape=[
            jax.ShapeDtypeStruct((pieces, pixels, wide), jnp.float32),
            jax.ShapeDtypeStruct((pieces, rows, wide), jnp.float32),
            jax.ShapeDtypeStruct((rows, pixels), jnp.bfloat16),
        ],
        scratch_shapes=[
            pltpu.VMEM((pixels // LANES, rows, LANES), jnp.float32),
            pltpu.VMEM((groups, rows, 1), jnp.float32),
        ],
        compiler_params=pltpu.CompilerParams(vmem_limit_bytes=60 * 1024 * 1024),
        cost_estimate=pl.CostEstimate(
            flops=2 * groups * pixels * rows * columns,
            bytes_accessed=groups * rows * columns * 2,
            transcendentals=0,
        ),
    )(x, live, who, my_scale, weights)


def cross_kernel(patch_ref, scale_ref, outs_ref, damp_ref, rhs_ref):
    scaled = (patch_ref[...].astype(jnp.float32) * scale_ref[...]).astype(jnp.bfloat16)
    cross = jnp.dot(scaled, outs_ref[0], preferred_element_type=jnp.float32)
    rhs_ref[...] = keep_off * cross + damp_ref[0]


def cross_call(patches, scale_row, outs, damp):
    rows, pixels = patches.shape
    pieces, _, wide = outs.shape
    return pl.pallas_call(
        cross_kernel,
        grid=(pieces,),
        in_specs=[
            pl.BlockSpec((rows, pixels), lambda n: (0, 0)),
            pl.BlockSpec((1, pixels), lambda n: (0, 0)),
            pl.BlockSpec((1, pixels, wide), lambda n: (n, 0, 0)),
            pl.BlockSpec((1, rows, wide), lambda n: (n, 0, 0)),
        ],
        out_specs=pl.BlockSpec((rows, wide), lambda n: (0, n)),
        out_shape=jax.ShapeDtypeStruct((rows, pieces * wide), jnp.float32),
        compiler_params=pltpu.CompilerParams(vmem_limit_bytes=60 * 1024 * 1024),
    )(patches, scale_row, outs, damp)


def body(activations, sample_count, client_weights):
    blk_count = lax.axis_size("blk")
    client_here = lax.axis_index("client")
    blk_here = lax.axis_index("blk")
    group_size, slot_count, rows_here, width, channels = activations.shape
    height = rows_here * blk_count
    client_total = sample_count.shape[0]
    client_groups = client_total // group_size
    stride = group_size * slot_count * width
    group_pixels = height * stride
    scale = 1.0 / (client_total * sample_count.astype(jnp.float32) * (height * width))

    shard = activations.transpose(2, 0, 1, 3, 4).reshape(rows_here * stride, channels)
    gathered = gather_call(shard, client_groups, blk_count).reshape(client_groups * group_pixels, channels)

    def per_pixel(value):
        value = value.reshape(client_groups, 1, group_size, slot_count, 1)
        full = jnp.broadcast_to(value, (client_groups, height, group_size, slot_count, width))
        return full.reshape(1, client_groups * group_pixels)

    slots = lax.broadcasted_iota(jnp.int32, (client_total, slot_count), 1)
    live = per_pixel((slots < sample_count[:, None]).astype(jnp.float32))
    scale_row = per_pixel(jnp.broadcast_to(scale[:, None], (client_total, slot_count)))
    member = lax.broadcasted_iota(jnp.int32, (client_total, slot_count), 0) % group_size
    who = per_pixel(member)[:, :group_pixels]

    tile = channels // blk_count
    mine = tile // client_groups
    first = blk_here * tile
    own = first + client_here * mine
    start = client_here * group_pixels
    own_x = lax.dynamic_slice_in_dim(gathered, own, mine, 1).T
    group_x = lax.dynamic_slice(gathered, (start, first), (group_pixels, tile)).T
    my_live = lax.dynamic_slice_in_dim(live, start, group_pixels, 1)
    my_scale_row = lax.dynamic_slice_in_dim(scale_row, start, group_pixels, 1)
    my_scale = lax.dynamic_slice_in_dim(scale, client_here * group_size, group_size)

    columns = client_weights.shape[2]
    pieces = columns // 256 if columns % 256 == 0 else 1
    partial_out, damp, patches = local_call(
        group_x, my_live, who, my_scale, client_weights, pieces, height, stride, width
    )
    wide = columns // pieces
    outs = reduce_call(partial_out.reshape(pieces, blk_count // 2, 2, group_pixels // blk_count, wide))
    rhs = cross_call(patches, my_scale_row, outs.reshape(pieces, group_pixels, wide), damp)

    core, side = client_here % 2, client_here // 2
    rhs = rhs.reshape(client_groups // 2, 2, mine * 9, columns)
    away = lax.dynamic_index_in_dim(rhs, 1 - core, 1, False).astype(jnp.bfloat16)
    keep = lax.dynamic_index_in_dim(rhs, core, 1, False)
    back = lax.ppermute(away, "client", [(c, c + 1 - 2 * (c % 2)) for c in range(client_groups)])
    keep = keep + back.astype(jnp.float32)
    away = lax.dynamic_index_in_dim(keep, 1 - side, 0, False).astype(jnp.bfloat16)
    keep = lax.dynamic_index_in_dim(keep, side, 0, False)
    back = lax.ppermute(away, "client", [(c, (c + 2) % client_groups) for c in range(client_groups)])

    gram = gram_call(
        (own * 9).astype(jnp.int32)[None], gathered, own_x, scale_row, live, height, stride, width
    )
    return gram, keep + back.astype(jnp.float32)


def solution(mesh):
    in_specs = (P("client", None, "blk", None, None), P(), P("client", "blk", None))
    out_specs = (P(("blk", "client"), None), P(("blk", "client"), None))
    return jax.shard_map(body, mesh=mesh, in_specs=in_specs, out_specs=out_specs, check_vma=False)
```

time: 270 us -> 136 us (0.50)
  waiting for transfers between devices: 194 us -> 4.14 us
  Pallas kernels: 37 us -> 109 us
  between operations: 13.8 us -> 0.76 us
  matrix products: 4.55 us -> 0 us
    all_gather x2 -> x0, waiting for transfers between devices: 122 us -> none  [the longest x1 61.3 us: body(): lax.all_gather(activations, ('client', 'blk'), axis=0, tiled=False)]
    pallas_call x2 -> x5, Pallas kernels: 37 us -> 109 us  [the longest x1 35.6 us: reduce_call(): pl.pallas_call(reduce_kernel, in_specs=[pl.BlockSpec(memory_space=pltpu.V...]
    reduce_scatter x2 -> x0, waiting for transfers between devices: 71.2 us -> none  [the longest x1 58.6 us: body(): lax.psum_scatter(partial_out, 'blk', scatter_dimension=0, tiled=True)]
    convert_element_type x2 -> x1, other arithmetic: 6.81 us -> 0.07 us  [body(): live = per_pixel((slots < sample_count[:, None]).astype(jnp.float32))]
    add x0 -> x2, other arithmetic: none -> 5.52 us  [the longest x1 2.95 us: body(): keep = keep + back.astype(jnp.float32)]
    unnamed x2 -> x18, local copies, waits for them, and re-layouts: 1.48 us -> 6.66 us
    dot_general x1 -> x0, matrix products: 4.55 us -> none  [body(): cross = jnp.dot(scaled, outs, preferred_element_type=jnp.float32)]
    convert_element_type x0 -> x2, local copies, waits for them, and re-layouts: none -> 4.47 us  [the longest x1 3.45 us: body(): lax.dynamic_index_in_dim(rhs, 1 - core, 1, False).astype(jnp.bfloat16)]
  transfers between devices with their start and end apart: 4 -> 2, of which waited for: 4 -> 1; matrix products, arithmetic and copies ran while one was open for 4% -> 1% of each run, Pallas kernels for 10% -> 20%
where the time goes in v2:
time: 136 us; the launch traced here: 135 us
  Pallas kernels  109 us (80%)
  local copies, waits for them, and re-layouts  14.5 us (11%)
  other arithmetic  6.34 us (5%)
  waiting for transfers between devices  4.14 us (3%)
    pallas_call x1, Pallas kernels, reduce_call(): pl.pallas_call(reduce_kernel, in_specs=[pl.BlockSpec(memory_space=pltpu.V...  35.6 us
    pallas_call x1, Pallas kernels, gram_call(): pl.pallas_call(functools.partial(gram_kernel, height, stride, width), gri...  27.7 us
    pallas_call x1, Pallas kernels, gather_call(): pl.pallas_call(gather_kernel, in_specs=[pl.BlockSpec(memory_space=pltpu.V...  24.9 us
    pallas_call x1, Pallas kernels, local_call(): pl.pallas_call(functools.partial(local_kernel, height, stride, width), gr...  11.8 us
    pallas_call x1, Pallas kernels, cross_call(): pl.pallas_call(cross_kernel, grid=(pieces,), in_specs=[pl.BlockSpec((rows...  8.98 us
    unnamed x18, local copies, waits for them, and re-layouts  6.66 us
    ppermute x1, waiting for transfers between devices, body(): lax.ppermute(away, 'client', [(c, c + 1 - 2 * (c % 2)) for c in range(cli...  4.14 us
    convert_element_type x1, local copies, waits for them, and re-layouts, body(): lax.dynamic_index_in_dim(rhs, 1 - core, 1, False).astype(jnp.bfloat16)  3.45 us
  transfers between devices with their start and end apart: 2, of which 1 were waited for; matrix products, arithmetic and copies ran while one was open for 1% of the time, Pallas kernels for 20%

profile of v2, /device:TPU:0, one launch (start us, length us, event | category | flops | bytes accessed | tf_op | source)
XLA Modules:
  0.0 135.3 jit_solution(12563851483122238693)
XLA Ops:
  0.7 0.7 multiply_divide_fusion
  1.3 0.7 lt.55
  2.1 0.1 broadcast_in_dim.11
  2.1 0.6 dynamic_slice.32.scale_ref
  2.7 0.1 compare_convert_fusion
  2.8 0.1 broadcast_select_fusion
  2.9 0.1 broadcast_in_dim.14
  3.0 0.1 reshape.88
  3.1 0.5 slice.4.who_ref
  3.6 0.1 broadcast_in_dim.13
  3.7 0.1 reshape.87.live_ref
  3.9 0.0 copy-start.6
  3.9 0.1 broadcast_in_dim.12
  4.0 0.1 reshape.86.scale_ref
  4.1 0.0 copy-start.7
  4.1 0.0 copy-start.3
  4.1 0.9 copy-done.3
  5.0 24.9 %shard_map.50 = bf16[4,8,32,1280]{3,2,1,0:T(8,128)(2,1)S(1)} custom-call(bf16[32,1280]{1,0:T(8,128)(2,1)S(1)} %bitcast.25), custom_call_target="tpu_custom_call" | custom-call | tf_op jit(solution)/shard_map/pallas_call | solution.py:190
  29.9 0.0 copy-start
  29.9 0.1 dynamic_slice.30
  30.0 1.1 copy.12
  31.1 0.5 constant_dynamic-slice_fusion
  31.6 11.8 %shard_map.52 = (f32[5,256,256]{2,1,0:T(8,128)}, f32[5,1440,256]{2,1,0:T(8,128)}, bf16[1440,256]{1,0:T(8,128)(2,1)}) custom-call(bf16[160,256]{1,0:T(8,128)(2,1)} %bitcast.28, f32[1,256]{1,0:T(1,128)} %get-tuple-element.9.live_ref, s32[1,256]{1,0:T(1,128)} %slice.4.who_ref, f32[2]{0:T(128)} %dynamic_slice.32.scale_ref, bf16[2,1440,1280]{2,1,0:T(8,128)(2,1)} %w_ref.1), custom_call_target="tpu_custom_call" | custom-call | flops 1887436800 | bytes 7372800 | tf_op jit(solution)/shard_map/pallas_call | solution.py:418
  43.4 0.0 copy-done.6
  43.4 0.0 copy-done.7
  43.4 0.0 copy-start.2
  43.5 1.3 copy-done.2
  44.8 35.6 %shard_map.53 = bf16[5,4,2,32,256]{4,3,2,1,0:T(8,128)(2,1)S(1)} custom-call(f32[5,4,2,32,256]{4,3,2,1,0:T(8,128)S(1)} %bitcast.24), custom_call_target="tpu_custom_call" | custom-call | tf_op jit(solution)/shard_map/pallas_call | solution.py:289
  80.4 0.0 copy-start.1
  80.4 0.8 copy-done.1
  81.2 9.0 %shard_map.54 = f32[1440,1280]{1,0:T(8,128)} custom-call(bf16[1440,256]{1,0:T(8,128)(2,1)} %get-tuple-element.5.patch_ref, f32[1,256]{1,0:T(1,128)} %get-tuple-element.8.scale_ref, bf16[5,256,256]{2,1,0:T(8,128)(2,1)} %bitcast.23, f32[5,1440,256]{2,1,0:T(8,128)} %get-tuple-element.7.damp_ref), custom_call_target="tpu_custom_call" | custom-call | tf_op jit(solution)/shard_map/pallas_call | solution.py:460
  90.2 3.5 %fusion = bf16[2,360,1280]{2,1,0:T(8,128)(2,1)} fusion(f32[2,2,360,1280]{3,2,1,0:T(8,128)} %bitcast.26, s32[]{:T(128)S(6)} %select_n.56), kind=kLoop, calls=%fused_computation.2 | loop fusion | bytes 3686404 | tf_op jit(solution)/shard_map/convert_element_type | solution.py:523
  93.6 0.0 collective-permute-start
  93.7 4.1 %collective-permute-done = bf16[2,360,1280]{2,1,0:T(8,128)(2,1)} collective-permute-done((bf16[2,360,1280]{2,1,0:T(8,128)(2,1)}, bf16[2,360,1280]{2,1,0:T(8,128)(2,1)}, u32[]{:S(2)}, u32[]{:S(2)}) %collective-permute-start) | collective-permute-done | bytes 1843232 | tf_op jit(solution)/shard_map/ppermute | solution.py:525
  97.8 2.9 %bitcast_add_fusion = f32[2,360,1280]{2,1,0:T(8,128)S(1)} fusion(bf16[2,360,1280]{2,1,0:T(8,128)(2,1)} %collective-permute-done, f32[2,2,360,1280]{3,2,1,0:T(8,128)} %bitcast.27, s32[]{:T(128)S(6)} %select_n.55), kind=kLoop, calls=%fused_computation.1 | loop fusion | flops 1843200 | bytes 9216004 | tf_op jit(solution)/shard_map/add | solution.py:526
  100.7 0.0 copy-start.4
  100.8 1.8 %copy-done.4 = f32[2,360,1280]{2,1,0:T(8,128)} copy-done((f32[2,360,1280]{2,1,0:T(8,128)}, f32[2,360,1280]{2,1,0:T(8,128)S(1)}, u32[]{:S(2)}) %copy-start.4) | copy-done | bytes 3686424
  102.6 1.0 fusion.1
  103.6 0.6 collective-permute-start.1
  104.2 0.0 copy-done
  104.2 0.1 constant_dynamic-slice_fusion.2
  104.3 0.8 copy.11
  105.1 0.0 copy-start.5
  105.1 27.7 %shard_map.51 = f32[360,11520]{1,0:T(8,128)} custom-call(s32[1]{0:T(128)} %bitcast.first_ref, bf16[1024,1280]{1,0:T(8,128)(2,1)} %bitcast.22, bf16[40,1024]{1,0:T(8,128)(2,1)} %bitcast.29, f32[1,1024]{1,0:T(1,128)} %copy-done.7, f32[1,1024]{1,0:T(1,128)} %copy-done.6), custom_call_target="tpu_custom_call" | custom-call | flops 8493465600 | bytes 16588800 | tf_op jit(solution)/shard_map/pallas_call | solution.py:351
  132.8 0.0 collective-permute-done.1
  132.8 0.0 copy-done.5
  132.8 2.6 %bitcast_add_fusion.1 = f32[360,1280]{1,0:T(8,128)} fusion(bf16[360,1280]{1,0:T(8,128)(2,1)} %collective-permute-done.1, f32[2,360,1280]{2,1,0:T(8,128)S(1)} %copy-done.5, s32[]{:T(128)S(6)} %select_n.58), kind=kLoop, calls=%fused_computation.3 | loop fusion | flops 921600 | bytes 4608004 | tf_op jit(solution)/shard_map/add | solution.py:534
  (2 shorter events, 0.0 us)
Async XLA Ops:
  3.9 39.6 %copy-start.6 = (f32[1,1024]{1,0:T(1,128)}, f32[1,1024]{1,0:T(1,128)S(1)}, u32[]{:S(2)}) copy-start(f32[1,1024]{1,0:T(1,128)S(1)} %reshape.87.live_ref) | copy-start | bytes 12292
  4.1 39.3 %copy-start.7 = (f32[1,1024]{1,0:T(1,128)}, f32[1,1024]{1,0:T(1,128)S(1)}, u32[]{:S(2)}) copy-start(f32[1,1024]{1,0:T(1,128)S(1)} %reshape.86.scale_ref) | copy-start | bytes 12292
  4.1 0.9 copy-start.3
  29.9 74.3 %copy-start = (bf16[4,8,32,1280]{3,2,1,0:T(8,128)(2,1)}, bf16[4,8,32,1280]{3,2,1,0:T(8,128)(2,1)S(1)}, u32[]{:S(2)}) copy-start(bf16[4,8,32,1280]{3,2,1,0:T(8,128)(2,1)S(1)} %shard_map.50) | copy-start | bytes 7864324
  43.4 1.3 copy-start.2
  80.4 0.8 copy-start.1
  93.6 4.1 %collective-permute-start = (bf16[2,360,1280]{2,1,0:T(8,128)(2,1)}, bf16[2,360,1280]{2,1,0:T(8,128)(2,1)}, u32[]{:S(2)}, u32[]{:S(2)}) collective-permute-start(bf16[2,360,1280]{2,1,0:T(8,128)(2,1)} %fusion), channel_id=1, source_target_pairs={{0,8},{8,0},{16,24},{24,16},{1,9},{9,1},{17,25},{25,17},{2,10},{10... | collective-permute-start | bytes 5529608 | tf_op jit(solution)/shard_map/ppermute | solution.py:525
  100.7 1.8 %copy-start.4 = (f32[2,360,1280]{2,1,0:T(8,128)}, f32[2,360,1280]{2,1,0:T(8,128)S(1)}, u32[]{:S(2)}) copy-start(f32[2,360,1280]{2,1,0:T(8,128)S(1)} %bitcast_add_fusion) | copy-start | bytes 11059204
  103.6 29.2 %collective-permute-start.1 = (bf16[360,1280]{1,0:T(8,128)(2,1)}, bf16[360,1280]{1,0:T(8,128)(2,1)}, u32[]{:S(2)}, u32[]{:S(2)}) collective-permute-start(bf16[360,1280]{1,0:T(8,128)(2,1)} %fusion.1), channel_id=1, source_target_pairs={{0,16},{8,24},{16,0},{24,8},{1,17},{9,25},{17,1},{25,9},{2,18},{10... | collective-permute-start | bytes 2764808 | tf_op jit(solution)/shard_map/ppermute | solution.py:529
  105.1 27.7 %copy-start.5 = (f32[2,360,1280]{2,1,0:T(8,128)S(1)}, f32[2,360,1280]{2,1,0:T(8,128)}, u32[]{:S(2)}) copy-start(f32[2,360,1280]{2,1,0:T(8,128)} %copy-done.4) | copy-start | bytes 11059204

commit v3 on v2

v3 whole, which is shorter than its diff:
```python
import functools

import jax
import jax.numpy as jnp
from jax import lax
from jax.experimental import pallas as pl
from jax.experimental.pallas import tpu as pltpu
from jax.sharding import PartitionSpec as P

keep_off = 0.9
LANES = 128


MESH = pl.DeviceIdType.MESH


def pixel_rows(count_ref, base, pixels, groups, slots, height, stride, width):
    lane = lax.broadcasted_iota(jnp.int32, (1, pixels), 1)
    slot = (lane // width) % slots
    client = (lane // (height * stride)) * groups + (lane // (slots * width)) % groups
    count = jnp.zeros((1, pixels), jnp.int32)
    for index in range(pixels // (height * slots * width)):
        count = jnp.where(client == index, count_ref[base + index], count)
    live = jnp.where(slot < count, 1.0, 0.0)
    total = count_ref.shape[0] * height * width
    return live, 1.0 / (total * count.astype(jnp.float32))


def expand(base_of, live, channels, scratch, height, stride, width):
    pixels = live.shape[1]
    lane = lax.broadcasted_iota(jnp.int32, (1, pixels), 1)
    col = lane % width
    row = (lane // stride) % height

    def shifted(value, step, inside):
        return jnp.where(inside, pltpu.roll(value, (-step) % pixels, 1), 0.0)

    for first in range(0, channels, 16):
        size = min(16, channels - first)
        base = jnp.where(live > 0.0, base_of(first, size), 0.0)
        for b in range(3):
            if b == 1:
                across = base
            else:
                across = shifted(base, b - 1, (col + (b - 1) >= 0) & (col + (b - 1) < width))
            for a in range(3):
                if a == 1:
                    both = across
                else:
                    both = shifted(across, (a - 1) * stride, (row + (a - 1) >= 0) & (row + (a - 1) < height))
                for chunk in range(pixels // LANES):
                    scratch[chunk, pl.ds(first * 9 + 3 * a + b, size, stride=9), :] = both[
                        :, chunk * LANES : (chunk + 1) * LANES
                    ]


def gather_kernel(x_ref, out_ref, recv_sem, send_sem):
    clients, blks = out_ref.shape[:2]
    rows = out_ref.shape[2]
    depth = blks // 2
    client, blk = lax.axis_index("client"), lax.axis_index("blk")
    core_mate = client + 1 - 2 * (client % 2)
    x_mate = (client + 2) % clients
    z, y = blk // 2, blk % 2
    y_mate = blk + 1 - 2 * y
    core_dev, x_dev, y_dev = (core_mate, blk), (x_mate, blk), (client, y_mate)
    up_dev, down_dev = (client, blk + 2), (client, blk - 2)
    half = rows // 2

    barrier = pltpu.get_barrier_semaphore()
    for device in (core_dev, x_dev, y_dev):
        pl.semaphore_signal(barrier, inc=1, device_id=device, device_id_type=MESH)

    @pl.when(z + 1 < depth)
    def _():
        pl.semaphore_signal(barrier, inc=1, device_id=up_dev, device_id_type=MESH)

    @pl.when(z > 0)
    def _():
        pl.semaphore_signal(barrier, inc=1, device_id=down_dev, device_id_type=MESH)

    pl.semaphore_wait(barrier, 3 + jnp.where(z > 0, 1, 0) + jnp.where(z + 1 < depth, 1, 0))

    def copy(lane, c, b, device, part=None, own=False):
        where = (c, b) if part is None else (c, b, pl.ds(part * half, half))
        dst = out_ref.at[where]
        src = dst
        if own:
            src = x_ref
        if part is None:
            recv = recv_sem.at[0, c * blks + b]
        else:
            recv = recv_sem.at[part, c * blks + b]
        return pltpu.make_async_remote_copy(
            src_ref=src,
            dst_ref=dst,
            send_sem=send_sem.at[lane, c * blks + b],
            recv_sem=recv,
            device_id=device,
            device_id_type=MESH,
        )

    def along_z(offset):
        if offset == 0:
            return None
        level = z + offset
        return (level >= 0) & (level < depth)

    def guarded(offset, action):
        inside = along_z(offset)
        if inside is None:
            action(blk)
        else:
            pl.when(inside)(lambda: action(blk + 2 * offset))

    order = [0]
    for distance in range(1, depth):
        order += [-distance, distance]

    for offset in order:

        def first(b):
            own = offset == 0
            if not own:
                copy(0, client, b, core_dev).wait_recv()
            if offset <= 0:

                @pl.when(z + 1 < depth)
                def _():
                    copy(0, client, b, up_dev, own=own).start()

            if offset >= 0:

                @pl.when(z > 0)
                def _():
                    copy(1, client, b, down_dev, own=own).start()

            copy(2, client, b, x_dev, own=own).start()
            copy(3, client, b, y_dev, own=own).start()
            copy(4, client, b, core_dev, own=own).start()

        guarded(offset, first)

    def mate_of(b):
        return b + 1 - 2 * y

    for offset in order:

        def second(b):
            copy(0, x_mate, b, core_dev).wait_recv()
            copy(3, x_mate, b, y_dev, part=0).start()
            copy(4, x_mate, b, core_dev).start()
            copy(0, client, mate_of(b), core_dev).wait_recv()
            copy(2, client, mate_of(b), x_dev, part=1).start()
            copy(4, client, mate_of(b), core_dev).start()

        guarded(offset, second)

    for offset in order:

        def third(b):
            copy(0, x_mate, mate_of(b), core_dev, part=0).wait_recv()
            copy(0, x_mate, mate_of(b), core_dev, part=1).wait_recv()
            copy(4, x_mate, mate_of(b), core_dev).start()

        guarded(offset, third)

    for offset in order:

        def fourth(b):
            far = (core_mate + 2) % clients
            for c, bb in ((core_mate, b), (far, b), (core_mate, mate_of(b)), (far, mate_of(b))):
                copy(0, c, bb, core_dev).wait_recv()
            own = offset == 0
            if offset <= 0:

                @pl.when(z + 1 < depth)
                def _():
                    copy(0, client, b, up_dev, own=own).wait_send()

            if offset >= 0:

                @pl.when(z > 0)
                def _():
                    copy(1, client, b, down_dev, own=own).wait_send()

            copy(2, client, b, x_dev, own=own).wait_send()
            copy(3, client, b, y_dev, own=own).wait_send()
            copy(4, client, b, core_dev, own=own).wait_send()
            copy(3, x_mate, b, y_dev, part=0).wait_send()
            copy(4, x_mate, b, core_dev).wait_send()
            copy(2, client, mate_of(b), x_dev, part=1).wait_send()
            copy(4, client, mate_of(b), core_dev).wait_send()
            copy(4, x_mate, mate_of(b), core_dev).wait_send()

        guarded(offset, fourth)

    out_ref[client, blk] = x_ref[...]


def gather_call(x, clients, blks):
    return pl.pallas_call(
        gather_kernel,
        in_specs=[pl.BlockSpec(memory_space=pltpu.VMEM)],
        out_specs=pl.BlockSpec(memory_space=pltpu.VMEM),
        out_shape=jax.ShapeDtypeStruct((clients, blks) + x.shape, x.dtype),
        scratch_shapes=[
            pltpu.SemaphoreType.DMA((2, clients * blks)),
            pltpu.SemaphoreType.DMA((5, clients * blks)),
        ],
        compiler_params=pltpu.CompilerParams(
            collective_id=1, has_side_effects=True, vmem_limit_bytes=40 * 1024 * 1024
        ),
    )(x)


def rhs_kernel(
    height, stride, width, groups, slots, count_ref, x_ref, w_ref, keep_ref, away_ref,
    wbuf, wide, patch, scaled, square, part_ref, ybuf, sums, zbuf, obuf, rbuf, abuf, cbuf,
    ws, ys, yr, zs, zr, gs, gr, fs, fr, cs, cr,
):
    pieces, depth = part_ref.shape[:2]
    cols = part_ref.shape[4]
    pixels = x_ref.shape[1]
    tall = wide.shape[1]
    client, blk = lax.axis_index("client"), lax.axis_index("blk")
    z, y = blk // 2, blk % 2
    core, side = client % 2, client // 2
    other = 1 - y
    y_dev = (client, blk + 1 - 2 * y)
    core_dev = (client + 1 - 2 * core, blk)
    mine = keep_ref.shape[0]

    def level(d):
        return (z + d) % depth

    def z_dev(d):
        return (client, level(d) * 2 + y)

    def w_copy(q):
        return pltpu.make_async_copy(w_ref.at[:, :, pl.ds(q * cols, cols)], wbuf.at[q], ws.at[q])

    for q in range(pieces):
        w_copy(q).start()

    barrier = pltpu.get_barrier_semaphore()
    pl.semaphore_signal(barrier, inc=1, device_id=y_dev, device_id_type=MESH)
    pl.semaphore_signal(barrier, inc=1, device_id=core_dev, device_id_type=MESH)
    for d in range(1, depth):
        pl.semaphore_signal(barrier, inc=1, device_id=z_dev(d), device_id_type=MESH)

    live, scale = pixel_rows(count_ref, client * groups, pixels, groups, slots, height, stride, width)
    who = (lax.broadcasted_iota(jnp.int32, (1, pixels), 1) // (slots * width)) % groups
    expand(
        lambda first, size: x_ref[first : first + size, :].astype(jnp.float32),
        live, x_ref.shape[0], wide, height, stride, width,
    )
    for chunk in range(wide.shape[0]):
        span = slice(chunk * LANES, (chunk + 1) * LANES)
        value = wide[chunk]
        patch[:, span] = value.astype(jnp.bfloat16)
        scaled[:, span] = (value * scale[:, span]).astype(jnp.bfloat16)
    pl.semaphore_wait(barrier, depth + 1)

    def send(src, dst, send_sem, recv_sem, device):
        return pltpu.make_async_remote_copy(
            src_ref=src, dst_ref=dst, send_sem=send_sem, recv_sem=recv_sem, device_id=device, device_id_type=MESH
        )

    def y_copy(q):
        return send(part_ref.at[q, :, other], ybuf.at[q], ys.at[q], yr.at[q], y_dev)

    def z_copy(q, d):
        return send(sums.at[q, level(d)], zbuf.at[q, d], zs.at[q, d], zr.at[q, d], z_dev(d))

    def share(q, d, to):
        here = obuf.at[q, level(d), y]
        return send(here, here, gs.at[q, to], gr.at[q, to], z_dev(to))

    def forward(q, d, column):
        here = obuf.at[q, level(d), column]
        return send(here, here, fs.at[q, d], fr.at[q, level(d)], y_dev)

    def core_copy(q):
        return send(abuf.at[q], cbuf.at[q], cs.at[q], cr.at[q], core_dev)

    def multiply(q):
        w_copy(q).wait()
        total = None
        for group in range(groups):
            picked = jnp.where(who == group, patch[...].astype(jnp.float32), 0.0).astype(jnp.bfloat16)
            term = lax.dot_general(
                picked, wbuf[q, group], (((0,), (0,)), ((), ())), preferred_element_type=jnp.float32
            )
            total = term if total is None else total + term
        part_ref[q] = total.reshape(part_ref.shape[1:])
        y_copy(q).start()

    def damping():
        for group in range(groups):
            term = jnp.zeros((tall, 1), jnp.float32)
            for chunk in range(wide.shape[0]):
                span = slice(chunk * LANES, (chunk + 1) * LANES)
                value = wide[chunk]
                value = jnp.where(who[:, span] == group, value * value * scale[:, span], 0.0)
                term += jnp.sum(value, axis=1, keepdims=True)
            square[group] = term * (1.0 - keep_off)

    def damp(q):
        total = None
        for group in range(groups):
            term = square[group] * wbuf[q, group].astype(jnp.float32)
            total = term if total is None else total + term
        rbuf[q] = total

    def add_y(q):
        y_copy(q).wait_recv()
        for d in range(depth):
            sums[q, level(d)] = part_ref[q, level(d), y] + ybuf[q, level(d)]
        for d in range(1, depth):
            z_copy(q, d).start()

    def add_z(q):
        total = sums[q, z]
        for d in range(1, depth):
            z_copy(q, d).wait_recv()
            total = total + zbuf[q, d]
        obuf[q, z, y] = total.astype(jnp.bfloat16)
        for d in range(1, depth):
            share(q, 0, d).start()
        forward(q, 0, y).start()

    def pass_on(q):
        for d in range(1, depth):
            share(q, depth - d, d).wait_recv()
            forward(q, depth - d, y).start()

    def rows_of(q, holder):
        if mine % 8 == 0:
            return rbuf[q, pl.ds(pl.multiple_of(holder * mine, 8), mine), :]
        value = rbuf[q, :mine, :]
        for index in range(1, tall // mine):
            value = jnp.where(holder == index, rbuf[q, index * mine : (index + 1) * mine, :], value)
        return value

    def cross(q):
        for d in range(depth):
            forward(q, d, other).wait_recv()
        product = jnp.dot(scaled[...], obuf[q].reshape(pixels, cols), preferred_element_type=jnp.float32)
        rbuf[q] = rbuf[q] + keep_off * product
        for far in range(2):
            abuf[q, far] = rows_of(q, far * 2 + 1 - core).astype(jnp.bfloat16)
        core_copy(q).start()

    def finish(q):
        core_copy(q).wait_recv()
        span = slice(q * cols, (q + 1) * cols)
        keep_ref[:, span] = rows_of(q, client) + cbuf[q, side].astype(jnp.float32)
        far = 1 - side
        away = rows_of(q, far * 2 + core) + cbuf[q, far].astype(jnp.float32)
        away_ref[:, span] = away.astype(jnp.bfloat16)

    for q in range(pieces):
        multiply(q)
    damping()
    for step in range(pieces + 4):
        if step < pieces:
            add_y(step)
        if 0 <= step - 1 < pieces:
            add_z(step - 1)
        if step < pieces:
            damp(step)
        if 0 <= step - 2 < pieces:
            pass_on(step - 2)
        if 0 <= step - 3 < pieces:
            cross(step - 3)
        if 0 <= step - 4 < pieces:
            finish(step - 4)

    for q in range(pieces):
        y_copy(q).wait_send()
        core_copy(q).wait_send()
        for d in range(1, depth):
            z_copy(q, d).wait_send()
            share(q, 0, d).wait_send()
        for d in range(depth):
            forward(q, d, y).wait_send()


def rhs_call(counts, x, weights, blks, mine, slots, height, stride, width):
    channels, pixels = x.shape
    groups, tall, columns = weights.shape
    pieces = columns // 256 if columns % 256 == 0 else 1
    cols = columns // pieces
    depth = blks // 2
    rows = pixels // blks
    sem = pltpu.SemaphoreType.DMA
    hop = pltpu.VMEM((pieces, depth, rows, cols), jnp.float32)
    return pl.pallas_call(
        functools.partial(rhs_kernel, height, stride, width, groups, slots),
        in_specs=[
            pl.BlockSpec(memory_space=pltpu.SMEM),
            pl.BlockSpec(memory_space=pltpu.VMEM),
            pl.BlockSpec(memory_space=pl.ANY),
        ],
        out_specs=[pl.BlockSpec(memory_space=pltpu.VMEM)] * 2,
        out_shape=[
            jax.ShapeDtypeStruct((mine, columns), jnp.float32),
            jax.ShapeDtypeStruct((mine, columns), jnp.bfloat16),
        ],
        scratch_shapes=[
            pltpu.VMEM((pieces, groups, tall, cols), jnp.bfloat16),
            pltpu.VMEM((pixels // LANES, tall, LANES), jnp.float32),
            pltpu.VMEM((tall, pixels), jnp.bfloat16),
            pltpu.VMEM((tall, pixels), jnp.bfloat16),
            pltpu.VMEM((groups, tall, 1), jnp.float32),
            pltpu.VMEM((pieces, depth, 2, rows, cols), jnp.float32),
            hop,
            hop,
            hop,
            pltpu.VMEM((pieces, depth, 2, rows, cols), jnp.bfloat16),
            pltpu.VMEM((pieces, tall, cols), jnp.float32),
            pltpu.VMEM((pieces, 2, mine, cols), jnp.bfloat16),
            pltpu.VMEM((pieces, 2, mine, cols), jnp.bfloat16),
            sem((pieces,)),
            sem((pieces,)),
            sem((pieces,)),
        ]
        + [sem((pieces, depth))] * 6
        + [sem((pieces,))] * 2,
        compiler_params=pltpu.CompilerParams(
            collective_id=2, has_side_effects=True, vmem_limit_bytes=60 * 1024 * 1024
        ),
    )(counts, x, weights)


def gram_kernel(height, stride, width, groups, slots, first_ref, count_ref, x_ref, own_ref, gram_ref, wide, narrow, mine_wide, mine_ref, flipped):
    step = pl.program_id(0)
    chunks = wide.shape[0]

    live, scale = pixel_rows(count_ref, 0, x_ref.shape[0], groups, slots, height, stride, width)

    @pl.when(step == 0)
    def _():
        expand(
            lambda first, size: own_ref[first : first + size, :].astype(jnp.float32),
            live, own_ref.shape[0], mine_wide, height, stride, width,
        )
        for chunk in range(chunks):
            part = slice(chunk * LANES, (chunk + 1) * LANES)
            mine_ref[:, part] = (mine_wide[chunk] * scale[:, part]).astype(jnp.bfloat16)

    flipped[...] = x_ref[...].astype(jnp.float32).T
    expand(
        lambda first, size: flipped[first : first + size, :],
        live, flipped.shape[0], wide, height, stride, width,
    )
    for chunk in range(chunks):
        narrow[:, chunk * LANES : (chunk + 1) * LANES] = wide[chunk].astype(jnp.bfloat16)
    product = lax.dot_general(
        mine_ref[...], narrow[...], (((1,), (1,)), ((), ())), preferred_element_type=jnp.float32
    )
    where_diag = first_ref[0] - step * product.shape[1]
    on_diag = (
        lax.broadcasted_iota(jnp.int32, product.shape, 1)
        == lax.broadcasted_iota(jnp.int32, product.shape, 0) + where_diag
    )
    gram_ref[...] = jnp.where(on_diag, product, keep_off * product)


def gram_call(first_row, counts, x, own, groups, slots, height, stride, width):
    pixels, channels = x.shape
    mine = own.shape[0]
    tile = LANES
    return pl.pallas_call(
        functools.partial(gram_kernel, height, stride, width, groups, slots),
        grid=(channels // tile,),
        in_specs=[
            pl.BlockSpec(memory_space=pltpu.SMEM),
            pl.BlockSpec(memory_space=pltpu.SMEM),
            pl.BlockSpec((pixels, tile), lambda j: (0, j)),
            pl.BlockSpec((mine, pixels), lambda j: (0, 0)),
        ],
        out_specs=pl.BlockSpec((mine * 9, tile * 9), lambda j: (0, j)),
        out_shape=jax.ShapeDtypeStruct((mine * 9, channels * 9), jnp.float32),
        scratch_shapes=[
            pltpu.VMEM((pixels // LANES, tile * 9, LANES), jnp.float32),
            pltpu.VMEM((tile * 9, pixels), jnp.bfloat16),
            pltpu.VMEM((pixels // LANES, mine * 9, LANES), jnp.float32),
            pltpu.VMEM((mine * 9, pixels), jnp.bfloat16),
            pltpu.VMEM((tile, pixels), jnp.float32),
        ],
        compiler_params=pltpu.CompilerParams(vmem_limit_bytes=60 * 1024 * 1024),
        cost_estimate=pl.CostEstimate(
            flops=2 * mine * 9 * channels * 9 * pixels,
            bytes_accessed=mine * channels * 81 * 4,
            transcendentals=0,
        ),
    )(first_row, counts, x, own)


def body(activations, sample_count, client_weights):
    blk_count = lax.axis_size("blk")
    client_here = lax.axis_index("client")
    blk_here = lax.axis_index("blk")
    group_size, slot_count, rows_here, width, channels = activations.shape
    height = rows_here * blk_count
    client_groups = sample_count.shape[0] // group_size
    stride = group_size * slot_count * width
    group_pixels = height * stride

    shard = activations.transpose(2, 0, 1, 3, 4).reshape(rows_here * stride, channels)
    gathered = gather_call(shard, client_groups, blk_count).reshape(client_groups * group_pixels, channels)

    tile = channels // blk_count
    mine = tile // client_groups
    first = blk_here * tile
    own = first + client_here * mine
    own_x = lax.dynamic_slice_in_dim(gathered, own, mine, 1).T
    group_x = lax.dynamic_slice(gathered, (client_here * group_pixels, first), (group_pixels, tile)).T
    keep, away = rhs_call(
        sample_count, group_x, client_weights, blk_count, mine * 9, slot_count, height, stride, width
    )
    back = lax.ppermute(away, "client", [(c, (c + 2) % client_groups) for c in range(client_groups)])
    gram = gram_call(
        (own * 9).astype(jnp.int32)[None], sample_count, gathered, own_x,
        group_size, slot_count, height, stride, width,
    )
    return gram, keep + back.astype(jnp.float32)


def solution(mesh):
    in_specs = (P("client", None, "blk", None, None), P(), P("client", "blk", None))
    out_specs = (P(("blk", "client"), None), P(("blk", "client"), None))
    return jax.shard_map(body, mesh=mesh, in_specs=in_specs, out_specs=out_specs, check_vma=False)
```

time: 136 us -> 102 us (0.75)
  Pallas kernels: 109 us -> 94.7 us
  local copies, waits for them, and re-layouts: 14.5 us -> 2.91 us
  waiting for transfers between devices: 4.14 us -> 0.01 us
  other arithmetic: 6.34 us -> 2.56 us
    pallas_call x4 -> x2, Pallas kernels: 84.1 us -> 69.9 us  [the longest x1 41.9 us: rhs_call(): pl.pallas_call(functools.partial(rhs_kernel, height, stride, width, group...]
    convert_element_type x2 -> x0, local copies, waits for them, and re-layouts: 4.47 us -> none  [the longest x1 3.45 us: body(): lax.dynamic_index_in_dim(rhs, 1 - core, 1, False).astype(jnp.bfloat16)]
    ppermute x1 -> x0, waiting for transfers between devices: 4.14 us -> none  [body(): lax.ppermute(away, 'client', [(c, c + 1 - 2 * (c % 2)) for c in range(cli...]
    unnamed x18 -> x8, local copies, waits for them, and re-layouts: 6.66 us -> 2.64 us
    add x1 -> x0, other arithmetic: 2.95 us -> none  [body(): keep = keep + back.astype(jnp.float32)]
  transfers between devices with their start and end apart: 2 -> 1, of which waited for: 1 -> 0; matrix products, arithmetic and copies ran while one was open for 1% -> 1% of each run, Pallas kernels for 20% -> 27%
where the time goes in v3:
time: 102 us
  Pallas kernels  94.7 us (93%)
  local copies, waits for them, and re-layouts  2.91 us (3%)
  other arithmetic  2.56 us (3%)
  starting transfers between devices  1.19 us (1%)
    pallas_call x1, Pallas kernels, rhs_call(): pl.pallas_call(functools.partial(rhs_kernel, height, stride, width, group...  41.9 us
    pallas_call x1, Pallas kernels, gram_call(): pl.pallas_call(functools.partial(gram_kernel, height, stride, width, grou...  28 us
    pallas_call x1, Pallas kernels, gather_call(): pl.pallas_call(gather_kernel, in_specs=[pl.BlockSpec(memory_space=pltpu.V...  24.9 us
    unnamed x8, local copies, waits for them, and re-layouts  2.64 us
    add x1, other arithmetic, body(): return (gram, keep + back.astype(jnp.float32))  2.56 us
  transfers between devices with their start and end apart: 1, of which 0 were waited for; matrix products, arithmetic and copies ran while one was open for 1% of the time, Pallas kernels for 27%

profile of v3, /device:TPU:0, one launch (start us, length us, event | category | flops | bytes accessed | tf_op | source)
XLA Modules:
  0.0 102.1 jit_solution(16134145527862334445)
XLA Ops:
  0.6 0.0 copy-start.1
  0.6 0.9 copy-done.1
  1.5 24.9 %shard_map.50 = bf16[4,8,32,1280]{3,2,1,0:T(8,128)(2,1)S(1)} custom-call(bf16[32,1280]{1,0:T(8,128)(2,1)S(1)} %bitcast.8), custom_call_target="tpu_custom_call" | custom-call | tf_op jit(solution)/shard_map/pallas_call | solution.py:202
  26.4 0.0 copy-start
  26.4 0.1 dynamic_slice.7
  26.6 1.0 copy.10
  27.6 41.9 %shard_map.52 = (f32[360,1280]{1,0:T(8,128)}, bf16[360,1280]{1,0:T(8,128)(2,1)}) custom-call(s32[8]{0:T(128)} %count_ref.3, bf16[160,256]{1,0:T(8,128)(2,1)} %bitcast.9, bf16[2,1440,1280]{2,1,0:T(8,128)(2,1)} %w_ref.1), custom_call_target="tpu_custom_call" | custom-call | tf_op jit(solution)/shard_map/pallas_call | solution.py:399
  69.4 1.2 %collective-permute-start = (bf16[360,1280]{1,0:T(8,128)(2,1)}, bf16[360,1280]{1,0:T(8,128)(2,1)}, u32[]{:S(2)}, u32[]{:S(2)}) collective-permute-start(bf16[360,1280]{1,0:T(8,128)(2,1)} %get-tuple-element.5), channel_id=1, source_target_pairs={{0,16},{8,24},{16,0},{24,8},{1,17},{9,25},{17,1},{25,9},{2,18},{10... | collective-permute-start | bytes 2764808 | tf_op jit(solution)/shard_map/ppermute | solution.py:524
  70.6 0.0 copy-done
  70.6 0.1 constant_dynamic-slice_fusion
  70.8 0.8 copy.9
  71.5 0.0 copy-start.2
  71.5 28.0 %shard_map.51 = f32[360,11520]{1,0:T(8,128)} custom-call(s32[1]{0:T(128)} %bitcast.first_ref, s32[8]{0:T(128)} %count_ref.3, bf16[1024,1280]{1,0:T(8,128)(2,1)} %bitcast.7, bf16[40,1024]{1,0:T(8,128)(2,1)} %bitcast.10), custom_call_target="tpu_custom_call" | custom-call | flops 8493465600 | bytes 16588800 | tf_op jit(solution)/shard_map/pallas_call | solution.py:475
  99.5 0.0 collective-permute-done
  99.5 0.0 copy-done.2
  99.5 2.6 %convert_add_fusion = f32[360,1280]{1,0:T(8,128)} fusion(f32[360,1280]{1,0:T(8,128)S(1)} %copy-done.2, bf16[360,1280]{1,0:T(8,128)(2,1)} %collective-permute-done), kind=kLoop, calls=%fused_computation | loop fusion | flops 921600 | bytes 4608000 | tf_op jit(solution)/shard_map/add | solution.py:529
Async XLA Ops:
  0.6 0.9 copy-start.1
  26.4 44.2 %copy-start = (bf16[4,8,32,1280]{3,2,1,0:T(8,128)(2,1)}, bf16[4,8,32,1280]{3,2,1,0:T(8,128)(2,1)S(1)}, u32[]{:S(2)}) copy-start(bf16[4,8,32,1280]{3,2,1,0:T(8,128)(2,1)S(1)} %shard_map.50) | copy-start | bytes 7864324
  69.4 30.1 %collective-permute-start = (bf16[360,1280]{1,0:T(8,128)(2,1)}, bf16[360,1280]{1,0:T(8,128)(2,1)}, u32[]{:S(2)}, u32[]{:S(2)}) collective-permute-start(bf16[360,1280]{1,0:T(8,128)(2,1)} %get-tuple-element.5), channel_id=1, source_target_pairs={{0,16},{8,24},{16,0},{24,8},{1,17},{9,25},{17,1},{25,9},{2,18},{10... | collective-permute-start | bytes 2764808 | tf_op jit(solution)/shard_map/ppermute | solution.py:524
  71.5 28.0 %copy-start.2 = (f32[360,1280]{1,0:T(8,128)S(1)}, f32[360,1280]{1,0:T(8,128)}, u32[]{:S(2)}) copy-start(f32[360,1280]{1,0:T(8,128)} %get-tuple-element.4) | copy-start | bytes 5529604

commit v4 on v3

--- a/solution.py
+++ b/solution.py
@@ -450,6 +450,15 @@
             part = slice(chunk * LANES, (chunk + 1) * LANES)
             mine_ref[:, part] = (mine_wide[chunk] * scale[:, part]).astype(jnp.bfloat16)
 
+    product = lax.dot_general(
+        mine_ref[...], narrow[...], (((1,), (1,)), ((), ())), preferred_element_type=jnp.float32
+    )
+    where_diag = first_ref[0] - (step - 1) * product.shape[1]
+    on_diag = (
+        lax.broadcasted_iota(jnp.int32, product.shape, 1)
+        == lax.broadcasted_iota(jnp.int32, product.shape, 0) + where_diag
+    )
+    gram_ref[...] = jnp.where(on_diag, product, keep_off * product)
     flipped[...] = x_ref[...].astype(jnp.float32).T
     expand(
         lambda first, size: flipped[first : first + size, :],
@@ -457,15 +466,6 @@
     )
     for chunk in range(chunks):
         narrow[:, chunk * LANES : (chunk + 1) * LANES] = wide[chunk].astype(jnp.bfloat16)
-    product = lax.dot_general(
-        mine_ref[...], narrow[...], (((1,), (1,)), ((), ())), preferred_element_type=jnp.float32
-    )
-    where_diag = first_ref[0] - step * product.shape[1]
-    on_diag = (
-        lax.broadcasted_iota(jnp.int32, product.shape, 1)
-        == lax.broadcasted_iota(jnp.int32, product.shape, 0) + where_diag
-    )
-    gram_ref[...] = jnp.where(on_diag, product, keep_off * product)
 
 
 def gram_call(first_row, counts, x, own, groups, slots, height, stride, width):
@@ -474,14 +474,14 @@
     tile = LANES
     return pl.pallas_call(
         functools.partial(gram_kernel, height, stride, width, groups, slots),
-        grid=(channels // tile,),
+        grid=(channels // tile + 1,),
         in_specs=[
             pl.BlockSpec(memory_space=pltpu.SMEM),
             pl.BlockSpec(memory_space=pltpu.SMEM),
-            pl.BlockSpec((pixels, tile), lambda j: (0, j)),
+            pl.BlockSpec((pixels, tile), lambda j: (0, jnp.minimum(j, channels // tile - 1))),
             pl.BlockSpec((mine, pixels), lambda j: (0, 0)),
         ],
-        out_specs=pl.BlockSpec((mine * 9, tile * 9), lambda j: (0, j)),
+        out_specs=pl.BlockSpec((mine * 9, tile * 9), lambda j: (0, jnp.maximum(j - 1, 0))),
         out_shape=jax.ShapeDtypeStruct((mine * 9, channels * 9), jnp.float32),
         scratch_shapes=[
             pltpu.VMEM((pixels // LANES, tile * 9, LANES), jnp.float32),

time: 102 us -> 105 us (1.029)
  Pallas kernels: 94.7 us -> 97.7 us
    pallas_call x1, Pallas kernels: 28 us -> 31 us  [gram_call(): pl.pallas_call(functools.partial(gram_kernel, height, stride, width, grou...]
  transfers between devices with their start and end apart: 1 -> 1, of which waited for: 0 -> 0; matrix products, arithmetic and copies ran while one was open for 1% -> 1% of each run, Pallas kernels for 27% -> 29%
where the time goes in v4:
time: 105 us
  Pallas kernels  97.7 us (93%)
  local copies, waits for them, and re-layouts  2.91 us (3%)
  other arithmetic  2.56 us (2%)
  starting transfers between devices  1.19 us (1%)
    pallas_call x1, Pallas kernels, rhs_call(): pl.pallas_call(functools.partial(rhs_kernel, height, stride, width, group...  41.9 us
    pallas_call x1, Pallas kernels, gram_call(): pl.pallas_call(functools.partial(gram_kernel, height, stride, width, grou...  31 us
    pallas_call x1, Pallas kernels, gather_call(): pl.pallas_call(gather_kernel, in_specs=[pl.BlockSpec(memory_space=pltpu.V...  24.9 us
    unnamed x8, local copies, waits for them, and re-layouts  2.64 us
    add x1, other arithmetic, body(): return (gram, keep + back.astype(jnp.float32))  2.56 us
  transfers between devices with their start and end apart: 1, of which 0 were waited for; matrix products, arithmetic and copies ran while one was open for 1% of the time, Pallas kernels for 29%

profile of v4, /device:TPU:0, one launch (start us, length us, event | category | flops | bytes accessed | tf_op | source)
XLA Modules:
  0.0 105.1 jit_solution(2661110485010747326)
XLA Ops:
  0.6 0.0 copy-start.1
  0.6 0.9 copy-done.1
  1.5 24.9 %shard_map.50 = bf16[4,8,32,1280]{3,2,1,0:T(8,128)(2,1)S(1)} custom-call(bf16[32,1280]{1,0:T(8,128)(2,1)S(1)} %bitcast.8), custom_call_target="tpu_custom_call" | custom-call | tf_op jit(solution)/shard_map/pallas_call | solution.py:202
  26.4 0.0 copy-start
  26.4 0.1 dynamic_slice.7
  26.6 1.0 copy.10
  27.6 41.9 %shard_map.52 = (f32[360,1280]{1,0:T(8,128)}, bf16[360,1280]{1,0:T(8,128)(2,1)}) custom-call(s32[8]{0:T(128)} %count_ref.3, bf16[160,256]{1,0:T(8,128)(2,1)} %bitcast.9, bf16[2,1440,1280]{2,1,0:T(8,128)(2,1)} %w_ref.1), custom_call_target="tpu_custom_call" | custom-call | tf_op jit(solution)/shard_map/pallas_call | solution.py:399
  69.4 1.2 %collective-permute-start = (bf16[360,1280]{1,0:T(8,128)(2,1)}, bf16[360,1280]{1,0:T(8,128)(2,1)}, u32[]{:S(2)}, u32[]{:S(2)}) collective-permute-start(bf16[360,1280]{1,0:T(8,128)(2,1)} %get-tuple-element.5), channel_id=1, source_target_pairs={{0,16},{8,24},{16,0},{24,8},{1,17},{9,25},{17,1},{25,9},{2,18},{10... | collective-permute-start | bytes 2764808 | tf_op jit(solution)/shard_map/ppermute | solution.py:524
  70.6 0.0 copy-done
  70.6 0.1 constant_dynamic-slice_fusion
  70.8 0.8 copy.9
  71.5 0.0 copy-start.2
  71.5 31.0 %shard_map.51 = f32[360,11520]{1,0:T(8,128)} custom-call(s32[1]{0:T(128)} %bitcast.first_ref, s32[8]{0:T(128)} %count_ref.3, bf16[1024,1280]{1,0:T(8,128)(2,1)} %bitcast.7, bf16[40,1024]{1,0:T(8,128)(2,1)} %bitcast.10), custom_call_target="tpu_custom_call" | custom-call | flops 8493465600 | bytes 16588800 | tf_op jit(solution)/shard_map/pallas_call | solution.py:475
  102.5 0.0 collective-permute-done
  102.5 0.0 copy-done.2
  102.5 2.6 %convert_add_fusion = f32[360,1280]{1,0:T(8,128)} fusion(f32[360,1280]{1,0:T(8,128)S(1)} %copy-done.2, bf16[360,1280]{1,0:T(8,128)(2,1)} %collective-permute-done), kind=kLoop, calls=%fused_computation | loop fusion | flops 921600 | bytes 4608000 | tf_op jit(solution)/shard_map/add | solution.py:529
Async XLA Ops:
  0.6 0.9 copy-start.1
  26.4 44.2 %copy-start = (bf16[4,8,32,1280]{3,2,1,0:T(8,128)(2,1)}, bf16[4,8,32,1280]{3,2,1,0:T(8,128)(2,1)S(1)}, u32[]{:S(2)}) copy-start(bf16[4,8,32,1280]{3,2,1,0:T(8,128)(2,1)S(1)} %shard_map.50) | copy-start | bytes 7864324
  69.4 33.1 %collective-permute-start = (bf16[360,1280]{1,0:T(8,128)(2,1)}, bf16[360,1280]{1,0:T(8,128)(2,1)}, u32[]{:S(2)}, u32[]{:S(2)}) collective-permute-start(bf16[360,1280]{1,0:T(8,128)(2,1)} %get-tuple-element.5), channel_id=1, source_target_pairs={{0,16},{8,24},{16,0},{24,8},{1,17},{9,25},{17,1},{25,9},{2,18},{10... | collective-permute-start | bytes 2764808 | tf_op jit(solution)/shard_map/ppermute | solution.py:524
  71.5 31.0 %copy-start.2 = (f32[360,1280]{1,0:T(8,128)S(1)}, f32[360,1280]{1,0:T(8,128)}, u32[]{:S(2)}) copy-start(f32[360,1280]{1,0:T(8,128)} %get-tuple-element.4) | copy-start | bytes 5529604
